TPU v7x, 128 devices: a whole 4x4x4 slice. The times are simulated.
128 devices in a mesh: section: 2 (over x_hi), dp: 8 (over z, core), mp: 8 (over x_lo, y).
Axes of the slice: x: 4 (x_hi: 2, x_lo: 2; x = x_hi * 2 + x_lo), y: 4, z: 4, core: 2. Of those that a mesh axis runs over, the one named last changes fastest.
Arguments:
- inputs: bfloat16 [2, 16, 128, 4096], P('section', 'dp'), may hold values from -6 to 6
- norm_gains: bfloat16 [2, 4096], P('section'), may hold values from 0.5 to 1.5
- weights: bfloat16 [2, 4096, 4, 4096], P('section', 'dp', None, 'mp'), may hold values from -0.09375 to 0.09375
- cotangent: bfloat16 [16, 128, 4096], P('dp'), may hold values from -6 to 6
- lengths: int32 [2, 16], P(None, 'dp'), may hold values from 32 to 128, as said below
- dp_noise: float32 [2, 4096, 4, 4096], P('section', 'dp', None, 'mp'), may hold values from -6 to 6
Outputs:
- noisy_grad: float32 [2, 4096, 4, 4096], P('section', 'dp', None, 'mp')
- clip_scale: float32 [16], P('dp')
Inputs may be any that keep to these rules, and one draw needn't show every extreme that they name: `lengths`: the first example of each row has length 128.
All inputs are finite; a program needn't handle non-finite values.
Results may differ from a plain program's by a relative error of at most 0.024.
Values may be sent and summed in bfloat16 or wider, within the bound.
A program may use at most 256 MiB of HBM per device.

v0:
```python
import jax
import jax.numpy as jnp
from jax import lax
from jax.sharding import PartitionSpec as P

D = 4096
HEADS = 64
HEAD = 64


def from_partner(x, axis, distance):
    return lax.ppermute(x, axis, [(i, i ^ 1 << distance) for i in range(lax.axis_size(axis))])


def rms_norm(values_in, gain_row):
    value32 = values_in.astype(jnp.float32)
    inverse = lax.rsqrt(jnp.mean(value32 * value32, axis=-1, keepdims=True) + 1e-06)
    return (value32 * inverse * gain_row.astype(jnp.float32)).astype(jnp.bfloat16)


def project(left, right):
    return jnp.dot(left, right, preferred_element_type=jnp.float32).astype(jnp.bfloat16)


def attend(queries, key_proj, value_proj, key_mask):
    seq_len = queries.shape[0]
    query_heads = queries.reshape(seq_len, -1, HEAD)
    key_heads = key_proj.reshape(seq_len, -1, HEAD)
    value_heads = value_proj.reshape(seq_len, -1, HEAD)
    scores = jnp.einsum(
        "shd,thd->hst", query_heads, key_heads, preferred_element_type=jnp.float32
    ) * HEAD ** (-0.5)
    scores = jnp.where(key_mask[None, None, :], scores, -jnp.inf)
    attn_probs = jax.nn.softmax(scores, axis=-1)
    probs_low = attn_probs.astype(jnp.bfloat16)
    context = jnp.einsum("hst,thd->shd", probs_low, value_heads, preferred_element_type=jnp.float32)
    return (attn_probs, context.reshape(seq_len, -1).astype(jnp.bfloat16))


def attend_back(queries, key_proj, value_proj, attn_probs, grad_ctx):
    seq_len = queries.shape[0]
    query_heads = queries.reshape(seq_len, -1, HEAD)
    key_heads = key_proj.reshape(seq_len, -1, HEAD)
    value_heads = value_proj.reshape(seq_len, -1, HEAD)
    grad_heads = grad_ctx.reshape(seq_len, -1, HEAD)
    grad_probs = jnp.einsum(
        "shd,thd->hst", grad_heads, value_heads, preferred_element_type=jnp.float32
    )
    inner_sum = jnp.sum(grad_probs * attn_probs, axis=-1, keepdims=True)
    grad_scores = (attn_probs * (grad_probs - inner_sum) * HEAD ** (-0.5)).astype(jnp.bfloat16)
    probs_low = attn_probs.astype(jnp.bfloat16)
    grad_query = jnp.einsum(
        "hst,thd->shd", grad_scores, key_heads, preferred_element_type=jnp.float32
    )
    grad_key = jnp.einsum(
        "hst,shd->thd", grad_scores, query_heads, preferred_element_type=jnp.float32
    )
    grad_value = jnp.einsum(
        "hst,shd->thd", probs_low, grad_heads, preferred_element_type=jnp.float32
    )
    return (
        grad_query.reshape(seq_len, -1).astype(jnp.bfloat16),
        grad_key.reshape(seq_len, -1).astype(jnp.bfloat16),
        grad_value.reshape(seq_len, -1).astype(jnp.bfloat16),
    )


def gram(matrix):
    return jnp.dot(matrix, matrix.T, preferred_element_type=jnp.float32)


def ghost(normed, kv_rows, grad_query, grad_key, grad_value, grad_out, context):
    first = jnp.sum(gram(normed) * gram(grad_query))
    second = jnp.sum(gram(kv_rows) * (gram(grad_key) + gram(grad_value)))
    third = jnp.sum(gram(grad_out) * gram(context))
    return first + second + third


def get_row(buffer, index):
    return lax.dynamic_index_in_dim(buffer, index, 0, keepdims=False)


def put_row(buffer, value, index, valid):
    current = get_row(buffer, index)
    return lax.dynamic_update_index_in_dim(buffer, jnp.where(valid, value, current), index, 0)


def per_device(inputs, norm_gains, weights, cotangent, lengths, dp_noise):
    section_index = lax.axis_index("section")
    is_dec = section_index == 1
    micro_count = inputs.shape[1]
    seq_len = inputs.shape[2]
    width = inputs.shape[3]
    gathered = lax.all_gather(weights, "dp", axis=1, tiled=True)[0]
    inner_dev = gathered.shape[2]
    own_inputs = inputs[0]
    gain_row = norm_gains[0]
    positions = jnp.arange(seq_len)
    wide_zero = jnp.zeros((micro_count, seq_len, width), jnp.bfloat16)
    thin_zero = jnp.zeros((micro_count, seq_len, inner_dev), jnp.bfloat16)
    normed_buf, kv_buf, gout_buf = (wide_zero, wide_zero, wide_zero)
    query_buf, key_buf, value_buf, context_buf = (thin_zero, thin_zero, thin_zero, thin_zero)
    gq_buf, gk_buf, gv_buf = (thin_zero, thin_zero, thin_zero)
    probs_buf = jnp.zeros((micro_count, inner_dev // HEAD, seq_len, seq_len), jnp.float32)
    norm_parts = jnp.zeros((micro_count,), jnp.float32)
    incoming = jnp.zeros((seq_len, width), jnp.bfloat16)
    for step_num in range(micro_count + 2):
        fwd_mb = step_num - section_index
        fwd_ok = (fwd_mb >= 0) & (fwd_mb < micro_count)
        fwd_idx = jnp.clip(fwd_mb, 0, micro_count - 1)
        rows_now = get_row(own_inputs, fwd_idx)
        normed = rms_norm(rows_now, gain_row)
        kv_rows = jnp.where(is_dec, incoming, normed)
        queries = project(normed, gathered[:, 0])
        key_proj = project(kv_rows, gathered[:, 1])
        value_proj = project(kv_rows, gathered[:, 2])
        key_mask = positions < get_row(lengths[0], fwd_idx)
        attn_probs, context_new = attend(queries, key_proj, value_proj, key_mask)
        normed_buf = put_row(normed_buf, normed, fwd_idx, fwd_ok)
        kv_buf = put_row(kv_buf, kv_rows, fwd_idx, fwd_ok)
        query_buf = put_row(query_buf, queries, fwd_idx, fwd_ok)
        key_buf = put_row(key_buf, key_proj, fwd_idx, fwd_ok)
        value_buf = put_row(value_buf, value_proj, fwd_idx, fwd_ok)
        probs_buf = put_row(probs_buf, attn_probs, fwd_idx, fwd_ok)
        context_buf = put_row(context_buf, context_new, fwd_idx, fwd_ok)
        bwd_mb = step_num - 2 + section_index
        bwd_ok = (bwd_mb >= 0) & (bwd_mb < micro_count)
        bwd_idx = jnp.clip(bwd_mb, 0, micro_count - 1)
        dec_mask = (positions < get_row(lengths[1], bwd_idx)).astype(jnp.bfloat16)
        cot_rows = get_row(cotangent, bwd_idx) * dec_mask[:, None]
        grad_out = jnp.where(is_dec, cot_rows, incoming)
        grad_ctx = project(grad_out, gathered[:, 3])
        back_query = get_row(query_buf, bwd_idx)
        back_key = get_row(key_buf, bwd_idx)
        back_value = get_row(value_buf, bwd_idx)
        back_context = get_row(context_buf, bwd_idx)
        grad_query, grad_key, grad_value = attend_back(
            back_query, back_key, back_value, get_row(probs_buf, bwd_idx), grad_ctx
        )
        sq_part = ghost(
            get_row(normed_buf, bwd_idx),
            get_row(kv_buf, bwd_idx),
            grad_query,
            grad_key,
            grad_value,
            grad_out,
            back_context,
        )
        gout_buf = put_row(gout_buf, grad_out, bwd_idx, bwd_ok)
        gq_buf = put_row(gq_buf, grad_query, bwd_idx, bwd_ok)
        gk_buf = put_row(gk_buf, grad_key, bwd_idx, bwd_ok)
        gv_buf = put_row(gv_buf, grad_value, bwd_idx, bwd_ok)
        slot_hit = bwd_ok & (jnp.arange(micro_count) == bwd_idx)
        norm_parts = jnp.where(slot_hit, sq_part, norm_parts)
        if step_num < micro_count + 1:
            relay_term = lax.cond(
                is_dec,
                lambda: jnp.einsum(
                    "sj,dj->sd", grad_key, gathered[:, 1], preferred_element_type=jnp.float32
                )
                + jnp.einsum(
                    "sj,dj->sd", grad_value, gathered[:, 2], preferred_element_type=jnp.float32
                ),
                lambda: jnp.einsum(
                    "sj,dj->sd", context_new, gathered[:, 3], preferred_element_type=jnp.float32
                ),
            )
            residual = jnp.where(is_dec, 0.0, rows_now.astype(jnp.float32))
            summed_rows = lax.psum(relay_term.astype(jnp.bfloat16), "mp").astype(jnp.float32)
            payload = (summed_rows + residual).astype(jnp.bfloat16)
            incoming = from_partner(payload, "section", 0)
    sq_norm = lax.psum(norm_parts, ("section", "mp"))
    bound = jnp.sqrt(jnp.float32(8.0 * D * HEADS * HEAD))
    clip_scale = bound / (jnp.sqrt(sq_norm) + 0.01 * bound)
    totals = jnp.zeros((weights.shape[1] * lax.axis_size("dp"), 4, inner_dev), jnp.float32)
    for micro_num in range(micro_count):
        normed_cols = normed_buf[micro_num]
        kv_cols = kv_buf[micro_num]
        gout_cols = gout_buf[micro_num]
        stacked = jnp.stack(
            [
                jnp.einsum(
                    "sd,sj->dj", normed_cols, gq_buf[micro_num], preferred_element_type=jnp.float32
                ),
                jnp.einsum(
                    "sd,sj->dj", kv_cols, gk_buf[micro_num], preferred_element_type=jnp.float32
                ),
                jnp.einsum(
                    "sd,sj->dj", kv_cols, gv_buf[micro_num], preferred_element_type=jnp.float32
                ),
                jnp.einsum(
                    "sd,sj->dj",
                    gout_cols,
                    context_buf[micro_num],
                    preferred_element_type=jnp.float32,
                ),
            ],
            axis=1,
        )
        totals = totals + clip_scale[micro_num] * stacked
    summed = lax.psum_scatter(
        totals.astype(jnp.bfloat16), "dp", scatter_dimension=0, tiled=True
    ).astype(jnp.float32)
    examples_total = micro_count * lax.axis_size("dp")
    noisy_grad = (summed + dp_noise[0]) / examples_total
    return (noisy_grad[None], clip_scale)


def solution(mesh):
    placed = (
        P("section", "dp", None, None),
        P("section", None),
        P("section", "dp", None, "mp"),
        P("dp", None, None),
        P(None, "dp"),
        P("section", "dp", None, "mp"),
    )
    return jax.shard_map(
        per_device,
        mesh=mesh,
        in_specs=placed,
        out_specs=(P("section", "dp", None, "mp"), P("dp")),
        check_vma=False,
    )
```

profile of v0, /device:TPU:1, one launch (start us, length us, event | category | flops | bytes accessed | tf_op | source)
XLA Modules:
  0.0 845.7 jit_solution(15828079697014097432)
XLA Ops:
  7.2 3.3 copy.83
  24.2 2.9 fusion.165
  31.3 2.3 constant_dynamic-slice_fusion.9
  36.5 2.3 constant_dynamic-slice_fusion.1
  38.8 60.7 %all-gather.2.cloned.1.call-done = bf16[1,4096,4,512]{3,1,2,0:T(8,128)(2,1)} async-done(((bf16[1,512,4,512]{3,1,2,0:T(8,128)(2,1)}), bf16[1,4096,4,512]{3,1,2,0:T(8,128)(2,1)}) %all-gather.2.cloned.1.call-update) | async-done | bytes 16777232 | tf_op jit(solution)/shard_map/all_gather | solution.py:94
  99.5 3.3 fusion.125
  103.5 3.6 bitcast_dynamic-update-slice_fusion.20
  107.2 3.0 bitcast_dynamic-update-slice_fusion.21
  112.5 3.0 bitcast_dynamic-update-slice_fusion.19
  130.8 4.8 conditional.3
  130.8 4.8 fusion
  145.6 2.7 fusion.232
  148.2 63.0 %all-reduce.4.cloned.1.call-done = bf16[128,4096]{1,0:T(8,128)(2,1)} async-done(((bf16[128,4096]{1,0:T(8,128)(2,1)}), bf16[128,4096]{1,0:T(8,128)(2,1)}) %all-reduce.4.cloned.1.call-update) | async-done | bytes 1048592 | tf_op jit(solution)/shard_map/psum | solution.py:169
  211.2 3.8 fusion.60
  215.5 3.6 bitcast_dynamic-update-slice_fusion.17
  221.2 3.0 fusion.132
  224.9 2.4 collective-permute-start
  227.3 3.6 fusion.131
  242.6 2.8 collective-permute-done
  245.4 6.0 bitcast_dynamic-update-slice_fusion.5
  252.5 3.7 fusion.138
  259.8 2.6 fusion.380
  262.4 3.8 bitcast_dynamic-update-slice_fusion.16
  267.0 3.2 fusion.126
  291.9 2.2 convolution_bitcast_fusion.12
  299.0 4.9 conditional.4
  299.0 4.8 fusion.8
  307.5 2.6 fusion.227
  315.2 70.6 %all-reduce.6.cloned.1.call-done = bf16[128,4096]{1,0:T(8,128)(2,1)} async-done(((bf16[128,4096]{1,0:T(8,128)(2,1)}), bf16[128,4096]{1,0:T(8,128)(2,1)}) %all-reduce.6.cloned.1.call-update) | async-done | bytes 1048592 | tf_op jit(solution)/shard_map/psum | solution.py:169
  387.3 2.5 collective-permute-start.1
  389.8 2.6 fusion.168
  395.2 12.4 %collective-permute-done.1 = bf16[128,4096]{1,0:T(8,128)(2,1)S(1)} collective-permute-done((bf16[128,4096]{1,0:T(8,128)(2,1)S(1)}, bf16[128,4096]{1,0:T(8,128)(2,1)S(1)}, u32[]{:S(2)}, u32[]{:S(2)}) %collective-permute-start.1) | collective-permute-done | bytes 1048608 | tf_op jit(solution)/shard_map/ppermute | solution.py:12
  407.6 4.8 bitcast_dynamic-update-slice_fusion.4
  413.4 3.7 fusion.139
  420.7 2.7 fusion.381
  423.4 3.9 bitcast_dynamic-update-slice_fusion.13
  438.9 3.2 fusion.127
  449.7 2.2 convolution_bitcast_fusion.9
  460.9 4.8 conditional.5
  460.9 4.8 fusion.16
  466.3 2.7 fusion.222
  469.1 2.6 fusion.225
  476.4 72.0 %all-reduce.8.cloned.1.call-done = bf16[128,4096]{1,0:T(8,128)(2,1)} async-done(((bf16[128,4096]{1,0:T(8,128)(2,1)}), bf16[128,4096]{1,0:T(8,128)(2,1)}) %all-reduce.8.cloned.1.call-update) | async-done | bytes 1048592 | tf_op jit(solution)/shard_map/psum | solution.py:169
  550.0 2.9 collective-permute-start.2
  552.8 2.6 fusion.171
  558.3 12.4 %collective-permute-done.2 = bf16[128,4096]{1,0:T(8,128)(2,1)S(1)} collective-permute-done((bf16[128,4096]{1,0:T(8,128)(2,1)S(1)}, bf16[128,4096]{1,0:T(8,128)(2,1)S(1)}, u32[]{:S(2)}, u32[]{:S(2)}) %collective-permute-start.2) | collective-permute-done | bytes 1048608 | tf_op jit(solution)/shard_map/ppermute | solution.py:12
  570.7 4.8 bitcast_dynamic-update-slice_fusion.3
  576.5 3.0 fusion.140
  581.9 4.0 bitcast_dynamic-update-slice_fusion.11
  585.9 3.6 fusion.128
  604.4 5.7 convolution_bitcast_fusion.1
  610.1 5.7 convolution_bitcast_fusion.5
  615.8 5.7 convolution_bitcast_fusion.2
  621.5 5.7 convolution_bitcast_fusion.6
  629.2 5.9 convolution_bitcast_fusion
  635.1 5.7 convolution_bitcast_fusion.4
  648.2 2.6 fusion.217
  654.0 5.7 convolution_bitcast_fusion.3
  662.1 5.8 convolution_bitcast_fusion.7
  667.9 31.8 %psum.31 = f32[2]{0:T(128)S(1)} all-reduce(f32[2]{0:T(128)S(1)} %and_select_fusion.3), channel_id=1, replica_groups=mesh['section'=2,'dp'=8,'mp'=8] {'section','mp'}, use_global_device_ids=true, to_apply=%region_37.38 | all-reduce | flops 2 | bytes 16 | tf_op jit(solution)/shard_map/psum | solution.py:172
  700.3 28.8 %fusion.33 = bf16[4096,4,512]{2,0,1:T(8,128)(2,1)} fusion(f32[4096,1,512]{2,0,1:T(8,128)} %convolution_bitcast_fusion.4, f32[4096,1,512]{2,0,1:T(8,128)} %convolution_bitcast_fusion.5, f32[4096,1,512]{2,0,1:T(8,128)} %convolution_bitcast_fusion.6, f32[4096,1,512]{2,0,1:T(8,128)} %convolution_bitcast_fusion.7, f32[4096,1,512]{2,0,1:T(8,128)} %convolution_bitcast_fusion, ...), kind=kLoop, calls=%fused_computation.37 | loop fusion | flops 83886080 | bytes 83886088 | tf_op jit(solution)/shard_map/convert_element_type | solution.py:202
  729.1 100.7 %reduce-scatter.2.cloned.1.call-done = bf16[512,4,512]{2,0,1:T(8,128)(2,1)} async-done(((bf16[4096,4,512]{2,0,1:T(8,128)(2,1)}), bf16[512,4,512]{2,0,1:T(8,128)(2,1)}) %reduce-scatter.2.cloned.1.call-update) | async-done | bytes 2097168 | tf_op jit(solution)/shard_map/reduce_scatter | solution.py:201
  829.9 4.4 fusion.35
  834.3 4.7 copy.145
  (274 shorter events, 177.5 us)
Async XLA Ops:
  7.2 92.3 %all-gather.2.cloned.1.call-start = ((), (), s32[]{:S(2)}) async-start(), calls=%async_computation.1 | async-start | bytes 18874368 | tf_op jit(solution)/shard_map/all_gather | solution.py:94
  10.6 0.7 copy-start.37
  10.6 0.8 copy-start.44
  10.6 2.1 copy-start
  10.6 200.7 %all-reduce.4.cloned.1.call-start = ((), (), s32[]{:S(2)}) async-start(), calls=%async_computation.2 | async-start | bytes 2097152 | tf_op jit(solution)/shard_map/psum | solution.py:169
  21.3 86.0 %copy-start.38 = (f32[128]{0:T(128)}, f32[128]{0:T(128)S(1)}, u32[]{:S(2)}) copy-start(f32[128]{0:T(128)S(1)} %add_rsqrt_fusion.3) | copy-start | bytes 1540
  22.9 4.3 copy-start.3
  110.2 6.1 copy-start.8
  110.3 2.2 copy-start.39
  115.5 5.8 copy-start.6
  129.1 1.7 copy-start.10
  135.6 250.2 %all-reduce.6.cloned.1.call-start = ((), (), s32[]{:S(2)}) async-start(), calls=%async_computation.3 | async-start | bytes 2097152 | tf_op jit(solution)/shard_map/psum | solution.py:169
  211.2 4.3 copy-start.36
  215.5 3.6 copy-start.43
  224.9 20.6 %collective-permute-start = (bf16[128,4096]{1,0:T(8,128)(2,1)}, bf16[128,4096]{1,0:T(8,128)(2,1)}, u32[]{:S(2)}, u32[]{:S(2)}) collective-permute-start(bf16[128,4096]{1,0:T(8,128)(2,1)} %get-tuple-element.111), channel_id=1, source_target_pairs={{0,64},{64,0},{1,65},{65,1},{2,66},{66,2},{3,67},{67,3},{4,68},{68... | collective-permute-start | bytes 3145736 | tf_op jit(solution)/shard_map/ppermute | solution.py:12
  251.5 1.0 copy-start.15
  252.5 5.3 copy-start.28
  273.4 3.9 copy-start.32
  282.3 3.4 copy-start.12
  282.3 3.4 copy-start.29
  282.3 4.5 copy-start.33
  282.3 4.5 copy-start.48
  303.9 244.5 %all-reduce.8.cloned.1.call-start = ((), (), s32[]{:S(2)}) async-start(), calls=%async_computation.4 | async-start | bytes 2097152 | tf_op jit(solution)/shard_map/psum | solution.py:169
  304.0 6.2 copy-start.1
  304.7 7.4 copy-start.22
  306.3 7.3 copy-start.21
  387.3 20.3 %collective-permute-start.1 = (bf16[128,4096]{1,0:T(8,128)(2,1)S(1)}, bf16[128,4096]{1,0:T(8,128)(2,1)S(1)}, u32[]{:S(2)}, u32[]{:S(2)}) collective-permute-start(bf16[128,4096]{1,0:T(8,128)(2,1)S(1)} %fusion.67), channel_id=1, source_target_pairs={{0,64},{64,0},{1,65},{65,1},{2,66},{66,2},{3,67},{67,3},{4,68},{68... | collective-permute-start | bytes 3145736 | tf_op jit(solution)/shard_map/ppermute | solution.py:12
  392.4 15.2 %copy-start.4 = (bf16[2,128,4096]{2,1,0:T(8,128)(2,1)S(1)}, bf16[2,128,4096]{2,1,0:T(8,128)(2,1)}, u32[]{:S(2)}) copy-start(bf16[2,128,4096]{2,1,0:T(8,128)(2,1)} %param.15) | copy-start | bytes 6291460
  392.4 15.2 %copy-start.42 = (f32[128]{0:T(128)S(1)}, f32[128]{0:T(128)}, u32[]{:S(2)}) copy-start(f32[128]{0:T(128)} %add_rsqrt_fusion.1) | copy-start | bytes 1540
  392.4 15.2 %copy-start.46 = (bf16[128]{0:T(256)(128)(2,1)S(1)}, bf16[128]{0:T(256)(128)(2,1)}, u32[]{:S(2)}) copy-start(bf16[128]{0:T(256)(128)(2,1)} %compare_convert_fusion.1) | copy-start | bytes 772
  412.4 1.0 copy-start.16
  413.4 5.3 copy-start.26
  423.4 5.6 copy-start.27
  445.3 2.2 copy-start.13
  445.3 2.5 copy-start.31
  465.7 6.0 copy-start.18
  465.7 364.2 %reduce-scatter.2.cloned.1.call-start = ((), (), s32[]{:S(2)}) async-start(), calls=%async_computation.5 | async-start | bytes 18874368 | tf_op jit(solution)/shard_map/reduce_scatter | solution.py:201
  466.3 7.0 copy-start.24
  466.3 8.5 %copy-start.23 = (bf16[1,128,512]{2,1,0:T(8,128)(2,1)S(1)}, bf16[1,128,512]{2,1,0:T(8,128)(2,1)}, u32[]{:S(2)}) copy-start(bf16[1,128,512]{2,1,0:T(8,128)(2,1)} %copy.138) | copy-start | bytes 393220
  550.0 20.7 %collective-permute-start.2 = (bf16[128,4096]{1,0:T(8,128)(2,1)S(1)}, bf16[128,4096]{1,0:T(8,128)(2,1)S(1)}, u32[]{:S(2)}, u32[]{:S(2)}) collective-permute-start(bf16[128,4096]{1,0:T(8,128)(2,1)S(1)} %fusion.77), channel_id=1, source_target_pairs={{0,64},{64,0},{1,65},{65,1},{2,66},{66,2},{3,67},{67,3},{4,68},{68... | collective-permute-start | bytes 3145736 | tf_op jit(solution)/shard_map/ppermute | solution.py:12
  555.5 15.2 %copy-start.5 = (bf16[2,128,4096]{2,1,0:T(8,128)(2,1)S(1)}, bf16[2,128,4096]{2,1,0:T(8,128)(2,1)}, u32[]{:S(2)}) copy-start(bf16[2,128,4096]{2,1,0:T(8,128)(2,1)} %param.15) | copy-start | bytes 6291460
  555.5 15.2 %copy-start.41 = (f32[128]{0:T(128)S(1)}, f32[128]{0:T(128)}, u32[]{:S(2)}) copy-start(f32[128]{0:T(128)} %add_rsqrt_fusion) | copy-start | bytes 1540
  555.5 15.2 %copy-start.45 = (bf16[128]{0:T(256)(128)(2,1)S(1)}, bf16[128]{0:T(256)(128)(2,1)}, u32[]{:S(2)}) copy-start(bf16[128]{0:T(256)(128)(2,1)} %compare_convert_fusion) | copy-start | bytes 772
  575.5 1.0 copy-start.14
  576.5 3.2 copy-start.25
  576.5 3.2 copy-start.47
  579.5 6.4 copy-start.30
  579.5 2.4 copy-start.7
  579.5 2.4 copy-start.35
  581.9 4.0 copy-start.2
  585.9 7.0 copy-start.9
  589.5 9.8 %copy-start.11 = (f32[1,8,128,128]{2,3,1,0:T(8,128)S(1)}, f32[1,8,128,128]{2,3,1,0:T(8,128)}, u32[]{:S(2)}) copy-start(f32[1,8,128,128]{2,3,1,0:T(8,128)} %constant_dynamic-slice_fusion.13) | copy-start | bytes 1572868
  595.5 5.5 copy-start.19
  595.5 5.5 copy-start.17
  621.5 5.7 copy-start.34
  635.1 9.2 %copy-start.20 = (bf16[8,64,128]{2,1,0:T(8,128)(2,1)S(1)}, bf16[8,64,128]{2,1,0:T(8,128)(2,1)}, u32[]{:S(2)}) copy-start(bf16[8,64,128]{2,1,0:T(8,128)(2,1)} %copy-done.19) | copy-start | bytes 393220
  699.7 29.4 %copy-start.40 = (f32[2]{0:T(128)}, f32[2]{0:T(128)S(1)}, u32[]{:S(2)}) copy-start(f32[2]{0:T(128)S(1)} %add_divide_fusion) | copy-start | bytes 28
Sparse Core Ops, SparseCore 0:
  10.7 88.7 all-gather.1
  135.7 75.4 all-reduce.3
  304.0 81.6 all-reduce.5
  465.8 82.5 all-reduce.7
  729.2 100.5 reduce-scatter.1
where the time goes:
time: 857 us; the launch traced here: 846 us
  waiting for transfers between devices  395 us (46%)
  matrix products  202 us (24%)
  other arithmetic  95.5 us (11%)
  local copies, waits for them, and re-layouts  91.1 us (11%)
  blocking collectives  31.8 us (4%)
  between operations  22.1 us (3%)
    psum x3, waiting for transfers between devices, per_device(): lax.psum(relay_term.astype(jnp.bfloat16), 'mp').astype(jnp.float32)  206 us
    reduce_scatter x1, waiting for transfers between devices, per_device(): lax.psum_scatter(totals.astype(jnp.bfloat16), 'dp', scatter_dimension=0,...  101 us
    all_gather x1, waiting for transfers between devices, per_device(): gathered = lax.all_gather(weights, 'dp', axis=1, tiled=True)[0]  60.7 us
    dot_general x16, matrix products, project(): jnp.dot(left, right, preferred_element_type=jnp.float32)  55 us
    dynamic_update_slice x25, other arithmetic, put_row(): lax.dynamic_update_index_in_dim(buffer, jnp.where(valid, value, current),...  45.1 us
    dot_general x28, matrix products, gram(): return jnp.dot(matrix, matrix.T, preferred_element_type=jnp.float32)  42.7 us
    dynamic_slice x35, local copies, waits for them, and re-layouts, get_row(): return lax.dynamic_index_in_dim(buffer, index, 0, keepdims=False)  37.2 us
    psum x1, blocking collectives, per_device(): sq_norm = lax.psum(norm_parts, ('section', 'mp'))  31.8 us
  transfers between devices with their start and end apart: 8, of which 8 were waited for; matrix products, arithmetic and copies ran while one was open for 10% of the time, Pallas kernels for 0%

commit v1 on v0

v1 whole, which is shorter than its diff:
```python
import functools

import jax
import jax.numpy as jnp
from jax import lax
from jax.experimental import pallas as pl
from jax.experimental.pallas import tpu as pltpu
from jax.sharding import PartitionSpec as P

D = 4096
HEADS = 64
HEAD = 64
MESH = pl.DeviceIdType.MESH
F32 = jnp.float32
BF16 = jnp.bfloat16
N = 8
ROWS = 256
PIECE = 512
CHUNKS = 4
CH = ROWS // CHUNKS
ANY = pl.BlockSpec(memory_space=pl.ANY)
HBM = pl.BlockSpec(memory_space=pltpu.HBM)
VM = pl.BlockSpec(memory_space=pltpu.VMEM)
SM = pl.BlockSpec(memory_space=pltpu.SMEM)
DMA = pltpu.SemaphoreType.DMA


def rc(src, dst, send_sem, recv_sem, dev):
    return pltpu.make_async_remote_copy(
        src_ref=src,
        dst_ref=dst,
        send_sem=send_sem,
        recv_sem=recv_sem,
        device_id=dev,
        device_id_type=MESH,
    )


def coords():
    return lax.axis_index("section"), lax.axis_index("dp"), lax.axis_index("mp")


def greet(devs, extra=None):
    barrier = pltpu.get_barrier_semaphore()
    for dev in devs:
        pl.semaphore_signal(barrier, inc=1, device_id=dev, device_id_type=MESH)
    if extra is not None:
        cond, dev = extra

        @pl.when(cond)
        def _():
            pl.semaphore_signal(barrier, inc=1, device_id=dev, device_id_type=MESH)

        pl.semaphore_wait(barrier, len(devs) + jnp.where(cond, 1, 0))
    else:
        pl.semaphore_wait(barrier, len(devs))


def mp_peers(s, d, m):
    return [(s, d, (m + i) % N) for i in range(1, N)]


def dp_near(s, d, m):
    return [(s, (d + 2) % N, m), (s, (d + 6) % N, m), (s, d + 1 - 2 * (d % 2), m)]


class DpGather:
    def __init__(self, count, own, dst, half, send, recv, local):
        self.n, self.own, self.dst, self.half = count, own, dst, half
        self.send, self.recv, self.local = send, recv, local
        s, d, m = coords()
        self.d = d
        self.left, self.right, self.far = (d + 6) % N, (d + 2) % N, (d + 4) % N
        self.sib = d + 1 - 2 * (d % 2)
        self.to_right, self.to_left = (s, self.right, m), (s, self.left, m)
        self.to_sib = (s, self.sib, m)

    def cp(self, j, kind, src, dst, dev):
        return rc(src, dst, self.send.at[j, kind], self.recv.at[j, kind], dev)

    def keep(self, j):
        return pltpu.make_async_copy(self.own(j), self.dst(j, self.d), self.local.at[j])

    def out(self, j, kind):
        d = self.d
        if kind == 0:
            return self.cp(j, 0, self.own(j), self.dst(j, d), self.to_right)
        if kind == 1:
            return self.cp(j, 1, self.own(j), self.dst(j, d), self.to_left)
        if kind == 2:
            ref = self.half(j, self.left, 0)
            return self.cp(j, 2, ref, ref, self.to_right)
        if kind == 3:
            ref = self.half(j, self.right, 1)
            return self.cp(j, 3, ref, ref, self.to_left)
        if kind == 4:
            return self.cp(j, 4, self.own(j), self.dst(j, d), self.to_sib)
        block = (self.left, self.right, self.far)[kind - 5]
        return self.cp(j, kind, self.dst(j, block), self.dst(j, block), self.to_sib)

    def into(self, j, kind):
        sib = self.sib
        if kind == 0:
            ref = self.dst(j, self.left)
        elif kind == 1:
            ref = self.dst(j, self.right)
        elif kind == 2:
            ref = self.half(j, self.far, 0)
        elif kind == 3:
            ref = self.half(j, self.far, 1)
        else:
            ref = self.dst(j, (sib, (sib + 6) % N, (sib + 2) % N, (sib + 4) % N)[kind - 4])
        return self.cp(j, kind, ref, ref, self.to_sib)

    def begin(self, j):
        self.out(j, 0).start()
        self.out(j, 1).start()
        self.out(j, 4).start()
        self.keep(j).start()

    def open(self):
        for j in range(min(2, self.n)):
            self.begin(j)

    def far_on(self, j):
        self.into(j, 2).wait_recv()
        self.into(j, 3).wait_recv()
        self.out(j, 7).start()

    def middle(self, j):
        self.into(j, 0).wait_recv()
        self.into(j, 1).wait_recv()
        self.out(j, 2).start()
        self.out(j, 3).start()
        self.out(j, 5).start()
        self.out(j, 6).start()
        if j + 2 < self.n:
            self.begin(j + 2)
        if j > 0:
            self.far_on(j - 1)

    def close(self):
        self.far_on(self.n - 1)
        for j in range(self.n):
            for kind in range(4, 8):
                self.into(j, kind).wait_recv()
            for kind in range(8):
                self.out(j, kind).wait_send()
            self.keep(j).wait()


class SliceGather:
    def __init__(self, source, turn, dest, send_t, recv_t, local_t, send, recv, local):
        s, d, m = coords()
        self.s, self.d, self.m = s, d, m
        self.source, self.turn, self.dest = source, turn, dest
        self.send_t, self.recv_t, self.local_t = send_t, recv_t, local_t
        self.send, self.recv, self.local = send, recv, local
        self.far = rc(source, turn, send_t, recv_t, (s, m, d))
        self.near = pltpu.make_async_copy(source, turn, local_t)

    def open(self):
        pl.when(self.d != self.m)(lambda: self.far.start())
        pl.when(self.d == self.m)(lambda: self.near.start())

    def rows(self, m):
        return self.dest.at[pl.ds(pl.multiple_of(m * ROWS, ROWS), ROWS)]

    def hand(self, i):
        return rc(
            self.turn,
            self.rows(self.m),
            self.send.at[i - 1],
            self.recv.at[i - 1],
            (self.s, self.d, (self.m + i) % N),
        )

    def taken(self, i):
        ref = self.rows((self.m + N - i) % N)
        return rc(ref, ref, self.send.at[i - 1], self.recv.at[i - 1], (self.s, self.d, (self.m + i) % N))

    def keep(self):
        return pltpu.make_async_copy(self.turn, self.rows(self.m), self.local)

    def middle(self):
        pl.when(self.d != self.m)(lambda: self.far.wait_recv())
        pl.when(self.d == self.m)(lambda: self.near.wait())
        for i in range(1, N):
            self.hand(i).start()
        self.keep().start()

    def close(self):
        for i in range(1, N):
            self.taken(i).wait_recv()
        for i in range(1, N):
            self.hand(i).wait_send()
        self.keep().wait()
        pl.when(self.d != self.m)(lambda: self.far.wait_send())


def piece(ref, m, rows=None):
    cols = pl.ds(pl.multiple_of(m * PIECE, PIECE), PIECE)
    if rows is None:
        return ref.at[:, cols]
    return ref.at[pl.ds(rows, CH), cols]


def gather_kernel(wt, xa, xb, full, slices, turn, w_send, w_recv, w_loc, t_send, t_recv, t_loc, b_send, b_recv, b_loc):
    s, d, m = coords()
    greet(mp_peers(s, d, m) + dp_near(s, d, m), (d != m, (s, m, d)))
    gather = DpGather(
        4,
        lambda j: wt.at[j],
        lambda j, b: full.at[j, b],
        lambda j, b, h: full.at[j, b, pl.ds(h * 256, 256)],
        w_send,
        w_recv,
        w_loc,
    )
    slots = [
        SliceGather(
            piece(ref, m),
            turn.at[i],
            slices.at[i],
            t_send.at[i],
            t_recv.at[i],
            t_loc.at[i],
            b_send.at[i],
            b_recv.at[i],
            b_loc.at[i],
        )
        for i, ref in enumerate((xa, xb))
    ]
    gather.open()
    slots[0].open()
    pl.when(s == 1)(slots[1].open)
    gather.middle(0)
    slots[0].middle()
    pl.when(s == 1)(slots[1].middle)
    for j in range(1, 4):
        gather.middle(j)
    gather.close()
    slots[0].close()
    pl.when(s == 1)(slots[1].close)


def gather_weights(wt, xa, xb):
    return pl.pallas_call(
        gather_kernel,
        name="gather_weights",
        out_shape=(
            jax.ShapeDtypeStruct((4, N, PIECE, PIECE), BF16),
            jax.ShapeDtypeStruct((3, N * ROWS, PIECE), BF16),
        ),
        in_specs=[VM, ANY, ANY],
        out_specs=(HBM, HBM),
        scratch_shapes=[
            pltpu.VMEM((2, ROWS, PIECE), BF16),
            DMA((4, 8)),
            DMA((4, 8)),
            DMA((4,)),
            DMA((2,)),
            DMA((2,)),
            DMA((2,)),
            DMA((2, 7)),
            DMA((2, 7)),
            DMA((2,)),
        ],
        compiler_params=pltpu.CompilerParams(collective_id=0, has_side_effects=True),
    )(wt, xa, xb)


class Relay:
    def __init__(self, first, terms, resid, total, recv_buf, own, res, summed, landed, sems):
        self.first, self.terms, self.resid, self.total = first, terms, resid, total
        self.recv_buf, self.own, self.res, self.summed, self.landed = recv_buf, own, res, summed, landed
        self.s_send, self.s_recv, self.h_send, self.h_recv, self.g_send, self.g_recv, self.loc = sems
        self.s, self.d, self.m = coords()
        self.partner = (1 - self.s, self.d, self.m)

    def peer(self, i):
        return (self.s, self.d, (self.m + i) % N)

    def scatter(self, c, i):
        return rc(
            piece(self.terms, (self.m + i) % N, c * CH),
            self.recv_buf.at[i - 1, pl.ds(c * CH, CH)],
            self.s_send.at[c, i - 1],
            self.s_recv.at[c, i - 1],
            self.peer(i),
        )

    def hand(self, c):
        rows = pl.ds(c * CH, CH)
        return rc(self.summed.at[rows], self.landed.at[rows], self.h_send.at[c], self.h_recv.at[c], self.partner)

    def spread(self, c, i):
        return rc(
            self.landed.at[pl.ds(c * CH, CH)],
            piece(self.total, self.m, c * CH),
            self.g_send.at[c, i - 1],
            self.g_recv.at[c, i - 1],
            self.peer(i),
        )

    def taken(self, c, i):
        ref = piece(self.total, (self.m + N - i) % N, c * CH)
        return rc(ref, ref, self.g_send.at[c, i - 1], self.g_recv.at[c, i - 1], self.peer(i))

    def keep(self, c):
        return pltpu.make_async_copy(
            self.landed.at[pl.ds(c * CH, CH)], piece(self.total, self.m, c * CH), self.loc.at[c]
        )

    def sender_open(self):
        for c in range(CHUNKS):
            for i in range(1, N):
                self.scatter(c, i).start()
        own = pltpu.make_async_copy(piece(self.terms, self.m), self.own, self.loc.at[0])
        own.start()
        if self.resid is not None:
            res = pltpu.make_async_copy(piece(self.resid, self.m), self.res, self.loc.at[1])
            res.start()
            res.wait()
        own.wait()

    def sender_rest(self):
        for c in range(CHUNKS):
            rows = pl.ds(c * CH, CH)
            for i in range(1, N):
                self.scatter(c, i).wait_recv()
            acc = self.own[rows].astype(F32)
            for i in range(1, N):
                acc = acc + self.recv_buf[i - 1, rows].astype(F32)
            if self.resid is not None:
                acc = acc + self.res[rows].astype(F32)
            self.summed[rows] = acc.astype(BF16)
            self.hand(c).start()
        for c in range(CHUNKS):
            for i in range(1, N):
                self.scatter(c, i).wait_send()
            self.hand(c).wait_send()

    def taker(self):
        for c in range(CHUNKS):
            self.hand(c).wait_recv()
            for i in range(1, N):
                self.spread(c, i).start()
            self.keep(c).start()
        for c in range(CHUNKS):
            for i in range(1, N):
                self.taken(c, i).wait_recv()
            for i in range(1, N):
                self.spread(c, i).wait_send()
            self.keep(c).wait()


RELAY_SCRATCH = [
    pltpu.VMEM((7, ROWS, PIECE), BF16),
    pltpu.VMEM((ROWS, PIECE), BF16),
    pltpu.VMEM((ROWS, PIECE), BF16),
    pltpu.VMEM((ROWS, PIECE), BF16),
    pltpu.VMEM((ROWS, PIECE), BF16),
    DMA((CHUNKS, 7)),
    DMA((CHUNKS, 7)),
    DMA((CHUNKS,)),
    DMA((CHUNKS,)),
    DMA((CHUNKS, 7)),
    DMA((CHUNKS, 7)),
    DMA((CHUNKS,)),
]


def forward_kernel(terms, resid, total, recv_buf, own, res, summed, landed, *sems):
    s, d, m = coords()
    greet(mp_peers(s, d, m) + [(1 - s, d, m)])
    relay = Relay(0, terms, resid, total, recv_buf, own, res, summed, landed, sems)

    @pl.when(s == 0)
    def _():
        relay.sender_open()
        relay.sender_rest()

    pl.when(s == 1)(relay.taker)


def relay_forward(terms, resid):
    return pl.pallas_call(
        forward_kernel,
        name="relay_forward",
        out_shape=jax.ShapeDtypeStruct((ROWS, D), BF16),
        in_specs=[ANY, ANY],
        out_specs=HBM,
        scratch_shapes=list(RELAY_SCRATCH),
        compiler_params=pltpu.CompilerParams(collective_id=1, has_side_effects=True),
    )(terms, resid)


def backward_kernel(terms, ctx, before, total, rights, recv_buf, own, res, summed, landed, *sems):
    s, d, m = coords()
    greet(mp_peers(s, d, m) + dp_near(s, d, m) + [(1 - s, d, m)])
    relay_sems, (y_send, y_recv, y_loc) = sems[:7], sems[7:]
    relay = Relay(1, terms, None, total, recv_buf, own, res, summed, landed, relay_sems)
    gather = DpGather(
        1,
        lambda j: ctx,
        lambda j, b: rights.at[3, pl.ds(pl.multiple_of(b * ROWS, ROWS), ROWS)],
        lambda j, b, h: rights.at[3, pl.ds(pl.multiple_of(b * ROWS + h * 128, 128), 128)],
        y_send,
        y_recv,
        y_loc,
    )
    pl.when(s == 1)(relay.sender_open)
    gather.open()
    pl.when(s == 1)(relay.sender_rest)
    gather.middle(0)
    gather.close()
    pl.when(s == 0)(relay.taker)


def relay_backward(terms, ctx, before):
    return pl.pallas_call(
        backward_kernel,
        name="relay_backward",
        out_shape=(
            jax.ShapeDtypeStruct((ROWS, D), BF16),
            jax.ShapeDtypeStruct((4, N * ROWS, PIECE), BF16),
        ),
        in_specs=[ANY, VM, HBM],
        out_specs=(HBM, HBM),
        scratch_shapes=list(RELAY_SCRATCH) + [DMA((1, 8)), DMA((1, 8)), DMA((1,))],
        input_output_aliases={2: 0},
        compiler_params=pltpu.CompilerParams(collective_id=2, has_side_effects=True),
    )(terms, ctx, before)


def final_kernel(
    gq, gk, gv, relayed, norm, slices_in, rights_in, slices, rights, norms,
    turn, norm_mp, norm_own, norm_far, norm_dp,
    y_send, y_recv, y_loc, t_send, t_recv, t_loc, b_send, b_recv, b_loc, n_send, n_recv, f_send, f_recv, e_send, e_recv,
):
    s, d, m = coords()
    dp_all = [(s, (d + i) % N, m) for i in range(1, N)]
    greet(mp_peers(s, d, m) + dp_all + [(1 - s, d, m)], (d != m, (s, m, d)))
    parts = (gq, gk, gv)
    gather = DpGather(
        3,
        lambda j: parts[j],
        lambda j, b: rights.at[j, pl.ds(pl.multiple_of(b * ROWS, ROWS), ROWS)],
        lambda j, b, h: rights.at[j, pl.ds(pl.multiple_of(b * ROWS + h * 128, 128), 128)],
        y_send,
        y_recv,
        y_loc,
    )
    slot = SliceGather(
        piece(relayed, m), turn, slices.at[2], t_send, t_recv, t_loc, b_send, b_recv, b_loc
    )

    def to_mp(i):
        return rc(norm, norm_mp.at[m], n_send.at[i - 1], n_recv.at[i - 1], (s, d, (m + i) % N))

    def from_mp(i):
        ref = norm_mp.at[(m + N - i) % N]
        return rc(ref, ref, n_send.at[i - 1], n_recv.at[i - 1], (s, d, (m + i) % N))

    def to_dp(i):
        return rc(norm_dp, norms.at[d], e_send.at[i - 1], e_recv.at[i - 1], (s, (d + i) % N, m))

    def from_dp(i):
        ref = norms.at[(d + N - i) % N]
        return rc(ref, ref, e_send.at[i - 1], e_recv.at[i - 1], (s, (d + i) % N, m))

    for i in range(1, N):
        to_mp(i).start()
    slot.open()
    gather.open()
    norm_mp[m] = norm[...]
    for i in range(1, N):
        from_mp(i).wait_recv()
    acc = norm_mp[0]
    for i in range(1, N):
        acc = acc + norm_mp[i]
    norm_own[...] = acc
    over = rc(norm_own, norm_far, f_send, f_recv, (1 - s, d, m))
    over.start()
    slot.middle()
    gather.middle(0)
    over.wait_recv()
    both = norm_own[...] + norm_far[...]
    norm_dp[...] = both
    norms[d] = both
    for i in range(1, N):
        to_dp(i).start()
    gather.middle(1)
    gather.middle(2)
    gather.close()
    slot.close()
    for i in range(1, N):
        from_dp(i).wait_recv()
    for i in range(1, N):
        to_mp(i).wait_send()
        to_dp(i).wait_send()
    over.wait_send()


def gather_grads(gq, gk, gv, relayed, norm, slices, rights):
    small = pltpu.VMEM((8, 128), F32)
    return pl.pallas_call(
        final_kernel,
        name="gather_grads",
        out_shape=(
            jax.ShapeDtypeStruct(slices.shape, BF16),
            jax.ShapeDtypeStruct(rights.shape, BF16),
            jax.ShapeDtypeStruct((N, 8, 128), F32),
        ),
        in_specs=[VM, VM, VM, ANY, VM, HBM, HBM],
        out_specs=(HBM, HBM, VM),
        scratch_shapes=[
            pltpu.VMEM((ROWS, PIECE), BF16),
            pltpu.VMEM((N, 8, 128), F32),
            small,
            small,
            small,
            DMA((3, 8)),
            DMA((3, 8)),
            DMA((3,)),
            DMA,
            DMA,
            DMA,
            DMA((7,)),
            DMA((7,)),
            DMA,
            DMA((7,)),
            DMA((7,)),
            DMA,
            DMA,
            DMA((7,)),
            DMA((7,)),
        ],
        input_output_aliases={5: 0, 6: 1},
        compiler_params=pltpu.CompilerParams(collective_id=3, has_side_effects=True),
    )(gq, gk, gv, relayed, norm, slices, rights)


def dot_nt(a, b):
    return lax.dot_general(a, b, (((1,), (1,)), ((), ())), preferred_element_type=F32)


def dot_nn(a, b):
    return lax.dot_general(a, b, (((1,), (0,)), ((), ())), preferred_element_type=F32)


def dot_tn(a, b):
    return lax.dot_general(a, b, (((0,), (0,)), ((), ())), preferred_element_type=F32)


def head_masks():
    lane = lax.broadcasted_iota(jnp.int32, (128, 128), 1)
    return lane < HEAD, lane >= HEAD


def soft(q, k, mask, key_ok):
    zero = jnp.zeros_like(q)
    scores = dot_nt(jnp.where(mask, q, zero), k) * HEAD ** (-0.5)
    scores = jnp.where(key_ok, scores, -jnp.inf)
    weights = jnp.exp(scores - jnp.max(scores, axis=-1, keepdims=True))
    return weights / jnp.sum(weights, axis=-1, keepdims=True)


def attend_kernel(lens, q_ref, k_ref, v_ref, ctx_ref):
    key_ok = lax.broadcasted_iota(jnp.int32, (128, 128), 1) < lens[pl.program_id(0)]
    masks = head_masks()
    for pair in range(4):
        cols = slice(pair * 128, pair * 128 + 128)
        q, k, v = q_ref[:, cols], k_ref[:, cols], v_ref[:, cols]
        zero = jnp.zeros_like(q)
        ctx = jnp.zeros((128, 128), F32)
        for mask in masks:
            probs = soft(q, k, mask, key_ok)
            ctx = ctx + dot_nn(probs.astype(BF16), jnp.where(mask, v, zero))
        ctx_ref[:, cols] = ctx.astype(BF16)


def attend(lens, q, k, v):
    spec = pl.BlockSpec((128, PIECE), lambda e: (e, 0))
    return pl.pallas_call(
        attend_kernel,
        name="attend",
        grid=(2,),
        in_specs=[SM] + [spec] * 3,
        out_specs=spec,
        out_shape=jax.ShapeDtypeStruct((ROWS, PIECE), BF16),
    )(lens, q, k, v)


def attend_all_kernel(lens, q_ref, k_ref, v_ref, g_ref, ctx_ref, gq_ref, gk_ref, gv_ref):
    key_ok = lax.broadcasted_iota(jnp.int32, (128, 128), 1) < lens[pl.program_id(0)]
    masks = head_masks()
    for pair in range(4):
        cols = slice(pair * 128, pair * 128 + 128)
        q, k, v, g = q_ref[:, cols], k_ref[:, cols], v_ref[:, cols], g_ref[:, cols]
        zero = jnp.zeros_like(q)
        ctx = gq = gk = gv = jnp.zeros((128, 128), F32)
        for mask in masks:
            probs = soft(q, k, mask, key_ok)
            low = probs.astype(BF16)
            g_one = jnp.where(mask, g, zero)
            gp = dot_nt(g_one, v)
            inner = jnp.sum(gp * probs, axis=-1, keepdims=True)
            gs = (probs * (gp - inner) * HEAD ** (-0.5)).astype(BF16)
            ctx = ctx + dot_nn(low, jnp.where(mask, v, zero))
            gq = gq + dot_nn(gs, jnp.where(mask, k, zero))
            gk = gk + dot_tn(gs, jnp.where(mask, q, zero))
            gv = gv + dot_tn(low, g_one)
        ctx_ref[:, cols] = ctx.astype(BF16)
        gq_ref[:, cols] = gq.astype(BF16)
        gk_ref[:, cols] = gk.astype(BF16)
        gv_ref[:, cols] = gv.astype(BF16)


def attend_all(lens, q, k, v, g):
    spec = pl.BlockSpec((128, PIECE), lambda e: (e, 0))
    shape = jax.ShapeDtypeStruct((ROWS, PIECE), BF16)
    return pl.pallas_call(
        attend_all_kernel,
        name="attend_all",
        grid=(2,),
        in_specs=[SM] + [spec] * 4,
        out_specs=(spec,) * 4,
        out_shape=(shape,) * 4,
    )(lens, q, k, v, g)


def norm_kernel(sec, xa, xb, xr, gq, gk, gv, ctx, out):
    example = pl.program_id(0)
    is_dec = sec[0] == 1

    def gram(ref):
        return dot_nt(ref[...], ref[...])

    kv, cc = gram(gk) + gram(gv), gram(ctx)
    none = jnp.zeros_like(cc)
    total = gram(xa) * (gram(gq) + jnp.where(is_dec, none, kv))
    total = total + gram(xr) * jnp.where(is_dec, kv, cc) + gram(xb) * jnp.where(is_dec, cc, none)
    value = jnp.sum(total)
    lane = lax.broadcasted_iota(jnp.int32, (8, 128), 1)
    mine = jnp.where(lane == example, value, 0.0)

    @pl.when(example == 0)
    def _():
        out[...] = mine

    @pl.when(example == 1)
    def _():
        out[...] += mine


def norm_parts(sec, xa, xb, xr, gq, gk, gv, ctx):
    wide = pl.BlockSpec((128, D), lambda e: (e, 0))
    thin = pl.BlockSpec((128, PIECE), lambda e: (e, 0))
    return pl.pallas_call(
        norm_kernel,
        name="norm_parts",
        grid=(2,),
        in_specs=[SM] + [wide] * 3 + [thin] * 4,
        out_specs=pl.BlockSpec((8, 128), lambda e: (0, 0)),
        out_shape=jax.ShapeDtypeStruct((8, 128), F32),
    )(sec, xa, xb, xr, gq, gk, gv, ctx)


BLOCK = 128


def weight_kernel(sec, clip, x_ref, y_ref, noise_ref, out_ref, scaled):
    @pl.when(pl.program_id(0) == 0)
    def _():
        for mat in range(4):

            @pl.loop(0, 16)
            def _(e):
                rows = pl.ds(pl.multiple_of(e * 128, 128), 128)
                scaled[mat, rows] = (y_ref[mat, rows].astype(F32) * clip[e]).astype(BF16)

    is_dec = sec[0]
    picks = (0, 2 * is_dec, 2 * is_dec, 2 - is_dec)
    for mat in range(4):
        total = dot_tn(x_ref[picks[mat]], scaled[mat])
        out_ref[:, mat, :] = (total + noise_ref[:, mat, :]) * (1.0 / 16.0)


def weight_grads(sec, clip, slices, rights, dp_noise):
    wide = pl.BlockSpec((BLOCK, 4, PIECE), lambda b: (b, 0, 0))
    return pl.pallas_call(
        weight_kernel,
        name="weight_grads",
        grid=(PIECE // BLOCK,),
        in_specs=[
            SM,
            SM,
            pl.BlockSpec((3, N * ROWS, BLOCK), lambda b: (0, 0, b)),
            pl.BlockSpec((4, N * ROWS, PIECE), lambda b: (0, 0, 0), pipeline_mode=pl.Buffered(1)),
            wide,
        ],
        out_specs=wide,
        out_shape=jax.ShapeDtypeStruct((PIECE, 4, PIECE), F32),
        scratch_shapes=[pltpu.VMEM((4, N * ROWS, PIECE), BF16)],
    )(sec, clip, slices, rights, dp_noise)


def rms_norm(values_in, gain_row):
    value32 = values_in.astype(F32)
    inverse = lax.rsqrt(jnp.mean(value32 * value32, axis=-1, keepdims=True) + 1e-06)
    return (value32 * inverse * gain_row.astype(F32)).astype(BF16)


def project(left, right):
    return jnp.dot(left, right, preferred_element_type=F32).astype(BF16)


def back_term(left, right):
    return jnp.einsum("sj,dj->sd", left, right, preferred_element_type=F32)


def per_device(inputs, norm_gains, weights, cotangent, lengths, dp_noise):
    section = lax.axis_index("section")
    is_dec = section == 1
    sec = jnp.reshape(section, (1,)).astype(jnp.int32)
    own_inputs = inputs[0].reshape(ROWS, D)
    normed = rms_norm(own_inputs, norm_gains[0])
    positions = jnp.arange(128)
    keep = (positions[None, :] < lengths[1][:, None]).astype(BF16)
    gout = (cotangent * keep[:, :, None]).reshape(ROWS, D)
    wt = jnp.swapaxes(weights[0], 0, 1)
    full, slices = gather_weights(wt, normed, gout)
    mats = full.reshape(4, D, PIECE)
    lens = lengths[0]
    thin = jnp.zeros((ROWS, PIECE), BF16)
    wide = jnp.zeros((ROWS, D), BF16)

    def first_dec():
        return project(normed, mats[0]), thin, thin, project(gout, mats[3]), thin, wide

    def first_enc():
        q, k, v = (project(normed, mats[i]) for i in range(3))
        ctx = attend(lens, q, k, v)
        return q, k, v, thin, ctx, back_term(ctx, mats[3]).astype(BF16)

    q, k, v, gctx, ctx, terms = lax.cond(is_dec, first_dec, first_enc)
    relayed = relay_forward(terms, own_inputs)

    def second_dec():
        k, v = project(relayed, mats[1]), project(relayed, mats[2])
        ctx, gq, gk, gv = attend_all(lens, q, k, v, gctx)
        terms = (back_term(gk, mats[1]) + back_term(gv, mats[2])).astype(BF16)
        return ctx, gq, gk, gv, terms

    def second_enc():
        return ctx, thin, thin, thin, wide

    ctx, gq, gk, gv, terms = lax.cond(is_dec, second_dec, second_enc)
    relayed, rights = relay_backward(terms, ctx, relayed)

    def third_dec():
        return gq, gk, gv

    def third_enc():
        _, gq, gk, gv = attend_all(lens, q, k, v, project(relayed, mats[3]))
        return gq, gk, gv

    gq, gk, gv = lax.cond(is_dec, third_dec, third_enc)
    norm = norm_parts(sec, normed, gout, relayed, gq, gk, gv, ctx)
    slices, rights, norms = gather_grads(gq, gk, gv, relayed, norm, slices, rights)
    sq_norm = norms[:, 0, :2]
    bound = jnp.sqrt(jnp.float32(8.0 * D * HEADS * HEAD))
    clip_all = bound / (jnp.sqrt(sq_norm) + 0.01 * bound)
    clip_scale = lax.dynamic_index_in_dim(clip_all, lax.axis_index("dp"), 0, keepdims=False)
    noisy_grad = weight_grads(sec, clip_all.reshape(16), slices, rights, dp_noise[0])
    return (noisy_grad[None], clip_scale)


def solution(mesh):
    placed = (
        P("section", "dp", None, None),
        P("section", None),
        P("section", "dp", None, "mp"),
        P("dp", None, None),
        P(None, "dp"),
        P("section", "dp", None, "mp"),
    )
    return jax.shard_map(
        per_device,
        mesh=mesh,
        in_specs=placed,
        out_specs=(P("section", "dp", None, "mp"), P("dp")),
        check_vma=False,
    )
```

time: 857 us -> 335 us (0.39); the launches traced: 846 us -> 334 us
  waiting for transfers between devices: 395 us -> 0 us
  Pallas kernels: 0 us -> 299 us
  matrix products: 202 us -> 17.9 us
  other arithmetic: 95.5 us -> 8.6 us
  local copies, waits for them, and re-layouts: 91.1 us -> 7.73 us
  blocking collectives: 31.8 us -> 0 us
  between operations: 22.1 us -> 0.81 us
    pallas_call x0 -> x8, Pallas kernels: none -> 299 us  [the longest x1 92.8 us: relay_backward(): pl.pallas_call(backward_kernel, name='relay_backward', out_shape=(jax.Sha...]
    psum x3 -> x0, waiting for transfers between devices: 206 us -> none  [per_device(): lax.psum(relay_term.astype(jnp.bfloat16), 'mp').astype(jnp.float32)]
    dot_general x79 -> x5, matrix products: 194 us -> 17.9 us  [the longest x4 14.4 us: project(): return jnp.dot(left, right, preferred_element_type=F32).astype(BF16)]
    reduce_scatter x1 -> x0, waiting for transfers between devices: 101 us -> none  [per_device(): lax.psum_scatter(totals.astype(jnp.bfloat16), 'dp', scatter_dimension=0,...]
    all_gather x1 -> x0, waiting for transfers between devices: 60.7 us -> none  [per_device(): gathered = lax.all_gather(weights, 'dp', axis=1, tiled=True)[0]]
    dynamic_update_slice x25 -> x0, other arithmetic: 45.1 us -> none  [put_row(): lax.dynamic_update_index_in_dim(buffer, jnp.where(valid, value, current),...]
    dynamic_slice x35 -> x0, local copies, waits for them, and re-layouts: 37.2 us -> none  [get_row(): return lax.dynamic_index_in_dim(buffer, index, 0, keepdims=False)]
    convert_element_type x7 -> x2, other arithmetic: 36.1 us -> 2.44 us  [the longest x1 2.37 us: rms_norm(): return (value32 * inverse * gain_row.astype(F32)).astype(BF16)]
  transfers between devices with their start and end apart: 8 -> 0, of which waited for: 8 -> 0; matrix products, arithmetic and copies ran while one was open for 10% -> 0% of each run, Pallas kernels for 0% -> 0%
where the time goes in v1:
time: 335 us; the launch traced here: 334 us
  Pallas kernels  299 us (89%)
  matrix products  17.9 us (5%)
  other arithmetic  8.6 us (3%)
  local copies, waits for them, and re-layouts  7.73 us (2%)
    pallas_call x1, Pallas kernels, relay_backward(): pl.pallas_call(backward_kernel, name='relay_backward', out_shape=(jax.Sha...  92.8 us
    pallas_call x1, Pallas kernels, gather_weights(): pl.pallas_call(gather_kernel, name='gather_weights', out_shape=(jax.Shape...  85.7 us
    pallas_call x1, Pallas kernels, gather_grads(): pl.pallas_call(final_kernel, name='gather_grads', out_shape=(jax.ShapeDty...  56.1 us
    pallas_call x1, Pallas kernels, relay_forward(): pl.pallas_call(forward_kernel, name='relay_forward', out_shape=jax.ShapeD...  35.8 us
    dot_general x4, matrix products, project(): return jnp.dot(left, right, preferred_element_type=F32).astype(BF16)  14.4 us
    pallas_call x1, Pallas kernels, weight_grads(): pl.pallas_call(weight_kernel, name='weight_grads', grid=(PIECE // BLOCK,)...  13.6 us

profile of v1, /device:TPU:1, one launch (start us, length us, event | category | flops | bytes accessed | tf_op | source)
XLA Modules:
  0.0 334.2 jit_solution(9996773034605166228)
XLA Ops:
  0.6 0.0 copy-start.11
  0.6 0.0 copy-start.5
  0.7 0.9 mul.42
  1.5 2.1 multiply_reduce_fusion
  3.6 0.0 copy-start.6
  3.6 2.4 multiply_convert_fusion.xa
  6.0 0.0 copy-done.11
  6.0 0.0 copy-start
  6.0 0.1 compare_convert_fusion
  6.1 0.0 copy-done.5
  6.1 1.7 broadcast_multiply_fusion
  7.9 0.0 copy-done.6
  7.9 1.7 copy.14
  9.6 85.7 %gather_weights.1 = (bf16[4,8,512,512]{3,2,1,0:T(8,128)(2,1)}, bf16[3,2048,512]{2,1,0:T(8,128)(2,1)}) custom-call(bf16[4,512,512]{2,1,0:T(8,128)(2,1)} %bitcast.79, bf16[256,4096]{1,0:T(8,128)(2,1)S(1)} %multiply_convert_fusion.xa, bf16[256,4096]{1,0:T(8,128)(2,1)} %bitcast.75), custom_call_target="tpu_custom_call" | custom-call | tf_op jit(solution)/shard_map/gather_weights/pallas_call | solution.py:248
  95.3 0.0 copy-done
  95.3 17.6 %conditional.4 = (bf16[256,512]{1,0:T(8,128)(2,1)S(1)}, bf16[256,512]{1,0:T(8,128)(2,1)S(1)}, bf16[256,512]{1,0:T(8,128)(2,1)S(1)}, bf16[256,512]{1,0:T(8,128)(2...) conditional(s32[]{:T(128)} %convert_element_type.53, (bf16[4,4096,512]{2,1,0:T(8,128)(2,1)}, ...), branch_computations={%region_1.0_spmd, %region_2.0_spmd} | conditional | flops 4296278016 | bytes 26476594
  95.3 3.4 %fusion.11.k_ref = bf16[256,512]{1,0:T(8,128)(2,1)S(1)} fusion(bf16[256,4096]{1,0:T(8,128)(2,1)S(1)} %get-tuple-element.49, bf16[4,4096,512]{2,1,0:T(8,128)(2,1)} %get-tuple-element.50), kind=kOutput, calls=%fused_computation.12 | convolution fusion | flops 1073872896 | bytes 6553600 | tf_op jit(solution)/shard_map/cond/branch_0_fun/dot_general | solution.py:717
  98.7 3.4 %fusion.14.v_ref = bf16[256,512]{1,0:T(8,128)(2,1)S(1)} fusion(bf16[256,4096]{1,0:T(8,128)(2,1)S(1)} %get-tuple-element.49, bf16[4,4096,512]{2,1,0:T(8,128)(2,1)} %get-tuple-element.50), kind=kOutput, calls=%fused_computation.13 | convolution fusion | flops 1073872896 | bytes 6553600 | tf_op jit(solution)/shard_map/cond/branch_0_fun/dot_general | solution.py:717
  102.2 3.4 %fusion.5.q_ref = bf16[256,512]{1,0:T(8,128)(2,1)S(1)} fusion(bf16[256,4096]{1,0:T(8,128)(2,1)S(1)} %get-tuple-element.49, bf16[4,4096,512]{2,1,0:T(8,128)(2,1)} %get-tuple-element.50), kind=kOutput, calls=%fused_computation.6 | convolution fusion | flops 1073741824 | bytes 6553600 | tf_op jit(solution)/shard_map/cond/branch_0_fun/dot_general | solution.py:717
  105.6 3.8 %attend.1 = bf16[256,512]{1,0:T(8,128)(2,1)S(1)} custom-call(s32[2]{0:T(128)S(1)} %get-tuple-element.51.lens, bf16[256,512]{1,0:T(8,128)(2,1)S(1)} %fusion.5.q_ref, bf16[256,512]{1,0:T(8,128)(2,1)S(1)} %fusion.11.k_ref, bf16[256,512]{1,0:T(8,128)(2,1)S(1)} %fusion.14.v_ref), custom_call_target="tpu_custom_call" | custom-call | tf_op jit(solution)/shard_map/cond/branch_0_fun/attend/pallas_call | solution.py:586
  109.4 3.5 %convolution_convert_fusion = bf16[256,4096]{1,0:T(8,128)(2,1)S(1)} fusion(bf16[256,512]{1,0:T(8,128)(2,1)S(1)} %attend.1, bf16[4,4096,512]{2,1,0:T(8,128)(2,1)} %get-tuple-element.50), kind=kOutput, calls=%fused_computation | convolution fusion | flops 1074790400 | bytes 6553600 | tf_op jit(solution)/shard_map/cond/branch_0_fun/sj,dj->sd/dot_general | solution.py:721
  112.9 0.0 copy-start.4
  112.9 0.0 copy-start.7
  113.0 0.0 copy-start.9
  113.0 1.3 copy-done.4
  114.3 35.8 %relay_forward.1.before = bf16[256,4096]{1,0:T(8,128)(2,1)S(1)} custom-call(bf16[256,4096]{1,0:T(8,128)(2,1)} %copy-done.4, bf16[256,4096]{1,0:T(8,128)(2,1)} %bitcast.78), custom_call_target="tpu_custom_call" | custom-call | tf_op jit(solution)/shard_map/relay_forward/pallas_call | solution.py:388
  150.1 0.0 copy-done.7
  150.1 0.0 copy-done.9
  150.1 3.0 conditional.5
  150.1 1.6 broadcast_in_dim.20
  151.7 0.7 broadcast_in_dim.14.clone
  152.4 0.7 broadcast_in_dim.14.clone.1
  153.2 0.0 copy-start.8
  153.2 0.0 copy-start.10
  153.2 92.8 %relay_backward.1 = (bf16[256,4096]{1,0:T(8,128)(2,1)S(1)}, bf16[4,2048,512]{2,1,0:T(8,128)(2,1)}) custom-call(bf16[256,4096]{1,0:T(8,128)(2,1)} %get-tuple-element.101.terms, bf16[256,512]{1,0:T(8,128)(2,1)S(1)} %get-tuple-element.102.ctx, bf16[256,4096]{1,0:T(8,128)(2,1)S(1)} %relay_forward.1.before), custom_call_target="tpu_custom_call", output_to_operand_aliasing={{0}: (2, {})} | custom-call | tf_op jit(solution)/shard_map/relay_backward/pallas_call | solution.py:422
  246.0 0.0 copy-done.8
  246.0 0.0 copy-done.10
  246.0 10.3 %conditional.6 = ((bf16[256,512]{1,0:T(8,128)(2,1)S(1)}, bf16[256,512]{1,0:T(8,128)(2,1)}, bf16[256,512]{1,0:T(8,128)(2,1)})) conditional(s32[]{:T(128)} %convert_element_type.53, (bf16[4,4096,512]{2,1,0:T(8,128)(2,1)}, bf16[256,4096]{1,0:T(8,128)(2,1)S(1)}, s32[2]{0:T(128)S(1)}, bf16[256,512]{1,0:T(8,128)(2,1)S(1)}, bf16[256,512]{1,0:T(8,128)(2,1)S(1)}, ...), branch_computations={%region_5.0_spmd, %region_6.0_spmd} | conditional | flops 1073872896 | bytes 6553632 | solution.py:770
  246.1 4.1 %fusion.47.g_ref = bf16[256,512]{1,0:T(8,128)(2,1)} fusion(bf16[256,4096]{1,0:T(8,128)(2,1)S(1)} %get-tuple-element.68, bf16[4,4096,512]{2,1,0:T(8,128)(2,1)} %get-tuple-element.69), kind=kOutput, calls=%fused_computation.39 | convolution fusion | flops 1073872896 | bytes 6553600 | tf_op jit(solution)/shard_map/cond/branch_0_fun/dot_general | solution.py:717
  250.2 6.2 %attend_all.3 = (bf16[256,512]{1,0:T(8,128)(2,1)}, bf16[256,512]{1,0:T(8,128)(2,1)S(1)}, bf16[256,512]{1,0:T(8,128)(2,1)}, bf16[256,512]{1,0:T(8,128)(2,1)}) custom-call(s32[2]{0:T(128)S(1)} %get-tuple-element.64.lens, bf16[256,512]{1,0:T(8,128)(2,1)S(1)} %get-tuple-element.65.q_ref, bf16[256,512]{1,0:T(8,128)(2,1)S(1)} %get-tuple-element.66.k_ref, ...), custom_call_target="tpu_custom_call" | custom-call | tf_op jit(solution)/shard_map/cond/branch_0_fun/attend_all/pallas_call | solution.py:624
  256.4 0.0 copy-start.3
  256.4 5.1 %norm_parts.1.norm = f32[8,128]{1,0:T(8,128)} custom-call(s32[1]{0:T(128)} %bitcast.9.sec, bf16[256,4096]{1,0:T(8,128)(2,1)} %copy-done, bf16[256,4096]{1,0:T(8,128)(2,1)} %bitcast.77, bf16[256,4096]{1,0:T(8,128)(2,1)S(1)} %get-tuple-element.103.xr.relayed, bf16[256,512]{1,0:T(8,128)(2,1)S(1)} %get-tuple-element.109.gq, ...), custom_call_target="tpu_custom_call" | custom-call | tf_op jit(solution)/shard_map/norm_parts/pallas_call | solution.py:661
  261.5 0.0 copy-done.3
  261.5 56.1 %gather_grads.1 = (bf16[3,2048,512]{2,1,0:T(8,128)(2,1)}, bf16[4,2048,512]{2,1,0:T(8,128)(2,1)}, f32[8,8,128]{2,1,0:T(8,128)}) custom-call(bf16[256,512]{1,0:T(8,128)(2,1)S(1)} %get-tuple-element.109.gq, bf16[256,512]{1,0:T(8,128)(2,1)S(1)} %copy-done.3, bf16[256,512]{1,0:T(8,128)(2,1)} %get-tuple-element.111.gv, ...), custom_call_target="tpu_custom_call", output_to_operand_aliasing={{0}: (5, {}), {1}: (6, {})} | custom-call | tf_op jit(solution)/shard_map/gather_grads/pallas_call | solution.py:508
  317.6 0.5 broadcast.51
  318.1 1.4 fusion.50
  319.5 0.6 div.17.clip
  320.1 13.6 %weight_grads.1 = f32[512,4,512]{2,1,0:T(4,128)} custom-call(s32[1]{0:T(128)} %bitcast.9.sec, f32[16]{0:T(128)} %div.17.clip, bf16[3,2048,512]{2,1,0:T(8,128)(2,1)} %get-tuple-element.115.x_ref, bf16[4,2048,512]{2,1,0:T(8,128)(2,1)} %get-tuple-element.116.y_ref, f32[512,4,512]{2,1,0:T(4,128)} %bitcast.84), custom_call_target="tpu_custom_call" | custom-call | tf_op jit(solution)/shard_map/weight_grads/pallas_call | solution.py:693
  333.7 0.5 dynamic-slice_bitcast_fusion
  (4 shorter events, 0.1 us)
Async XLA Ops:
  0.6 5.4 %copy-start.11 = (s32[2,2]{1,0:T(2,128)S(1)}, s32[2,2]{1,0:T(2,128)}, u32[]{:S(2)}) copy-start(s32[2,2]{1,0:T(2,128)} %param.16) | copy-start | bytes 52
  0.6 5.5 %copy-start.5 = (bf16[2,128,4096]{2,1,0:T(8,128)(2,1)S(1)}, bf16[2,128,4096]{2,1,0:T(8,128)(2,1)}, u32[]{:S(2)}) copy-start(bf16[2,128,4096]{2,1,0:T(8,128)(2,1)} %param.15) | copy-start | bytes 6291460
  3.6 4.2 %copy-start.6 = (bf16[1,512,4,512]{3,2,1,0:T(4,128)(2,1)S(1)}, bf16[1,512,4,512]{3,2,1,0:T(4,128)(2,1)}, u32[]{:S(2)}) copy-start(bf16[1,512,4,512]{3,2,1,0:T(4,128)(2,1)} %param.14) | copy-start | bytes 6291460
  6.0 89.3 %copy-start = (bf16[256,4096]{1,0:T(8,128)(2,1)}, bf16[256,4096]{1,0:T(8,128)(2,1)S(1)}, u32[]{:S(2)}) copy-start(bf16[256,4096]{1,0:T(8,128)(2,1)S(1)} %multiply_convert_fusion.xa) | copy-start | bytes 6291460
  112.9 1.3 copy-start.4
  112.9 37.2 %copy-start.7 = (bf16[256,512]{1,0:T(8,128)(2,1)}, bf16[256,512]{1,0:T(8,128)(2,1)S(1)}, u32[]{:S(2)}) copy-start(bf16[256,512]{1,0:T(8,128)(2,1)S(1)} %get-tuple-element.104) | copy-start | bytes 786436
  113.0 37.2 %copy-start.9 = (bf16[256,512]{1,0:T(8,128)(2,1)}, bf16[256,512]{1,0:T(8,128)(2,1)S(1)}, u32[]{:S(2)}) copy-start(bf16[256,512]{1,0:T(8,128)(2,1)S(1)} %get-tuple-element.105) | copy-start | bytes 786436
  153.2 92.9 %copy-start.8 = (bf16[256,512]{1,0:T(8,128)(2,1)S(1)}, bf16[256,512]{1,0:T(8,128)(2,1)}, u32[]{:S(2)}) copy-start(bf16[256,512]{1,0:T(8,128)(2,1)} %copy-done.7) | copy-start | bytes 786436
  153.2 92.9 %copy-start.10 = (bf16[256,512]{1,0:T(8,128)(2,1)S(1)}, bf16[256,512]{1,0:T(8,128)(2,1)}, u32[]{:S(2)}) copy-start(bf16[256,512]{1,0:T(8,128)(2,1)} %copy-done.9) | copy-start | bytes 786436
  256.4 5.1 %copy-start.3 = (bf16[256,512]{1,0:T(8,128)(2,1)S(1)}, bf16[256,512]{1,0:T(8,128)(2,1)}, u32[]{:S(2)}) copy-start(bf16[256,512]{1,0:T(8,128)(2,1)} %get-tuple-element.110.gk) | copy-start | bytes 786436

commit v2 on v1

--- a/solution.py
+++ b/solution.py
@@ -149,53 +149,104 @@
             self.keep(j).wait()
 
 
+class MpGather:
+    def __init__(self, chunks, source, slot, send, recv, local):
+        s, d, m = coords()
+        self.chunks, self.source, self.slot = chunks, source, slot
+        self.send, self.recv, self.local = send, recv, local
+        x, y = m // 4, m % 4
+        up, down, far = (y + 1) % 4, (y + 3) % 4, (y + 2) % 4
+        self.m, self.xm = m, (1 - x) * 4 + y
+        self.to = ((s, d, self.xm), (s, d, x * 4 + up), (s, d, x * 4 + down))
+        self.sources = (m, m, m, self.xm, self.xm, down, 4 + up)
+        self.landing = (
+            self.xm,
+            x * 4 + down,
+            x * 4 + up,
+            (1 - x) * 4 + down,
+            (1 - x) * 4 + up,
+            far,
+            4 + far,
+        )
+
+    def out(self, c, kind):
+        dest = self.slot(self.sources[kind], c)
+        src = self.source(c) if kind < 3 else dest
+        to = self.to[(0, 1, 2, 1, 2, 1, 2)[kind]]
+        return rc(src, dest, self.send.at[c, kind], self.recv.at[c, kind], to)
+
+    def into(self, c, kind):
+        ref = self.slot(self.landing[kind], c)
+        return rc(ref, ref, self.send.at[c, kind], self.recv.at[c, kind], self.to[0])
+
+    def keep(self, c):
+        return pltpu.make_async_copy(self.source(c), self.slot(self.m, c), self.local.at[c])
+
+    def stage(self, c, number):
+        if not 0 <= c < self.chunks:
+            return
+        waits, starts = (((), (0, 1, 2)), ((0,), (3, 4)), ((1, 2, 3, 4), (5, 6)), ((5, 6), ()))[number]
+        for kind in waits:
+            self.into(c, kind).wait_recv()
+        for kind in starts:
+            self.out(c, kind).start()
+        if number == 0:
+            self.keep(c).start()
+
+    def close(self):
+        for c in range(self.chunks):
+            for kind in range(7):
+                self.out(c, kind).wait_send()
+            self.keep(c).wait()
+
+
+def mp_near(s, d, m):
+    x, y = m // 4, m % 4
+    return [(s, d, (1 - x) * 4 + y), (s, d, x * 4 + (y + 1) % 4), (s, d, x * 4 + (y + 3) % 4)]
+
+
+SLICE_CHUNKS = 2
+
+
 class SliceGather:
     def __init__(self, source, turn, dest, send_t, recv_t, local_t, send, recv, local):
         s, d, m = coords()
-        self.s, self.d, self.m = s, d, m
-        self.source, self.turn, self.dest = source, turn, dest
-        self.send_t, self.recv_t, self.local_t = send_t, recv_t, local_t
-        self.send, self.recv, self.local = send, recv, local
-        self.far = rc(source, turn, send_t, recv_t, (s, m, d))
-        self.near = pltpu.make_async_copy(source, turn, local_t)
+        self.d, self.m = d, m
+        self.far = lambda: rc(source, turn, send_t, recv_t, (s, m, d))
+        self.near = lambda: pltpu.make_async_copy(source, turn, local_t)
+        step = ROWS // SLICE_CHUNKS
+        self.gather = MpGather(
+            SLICE_CHUNKS,
+            lambda c: turn.at[pl.ds(c * step, step)],
+            lambda mm, c: dest.at[pl.ds(pl.multiple_of(mm * ROWS + c * step, step), step)],
+            send,
+            recv,
+            local,
+        )
 
     def open(self):
-        pl.when(self.d != self.m)(lambda: self.far.start())
-        pl.when(self.d == self.m)(lambda: self.near.start())
-
-    def rows(self, m):
-        return self.dest.at[pl.ds(pl.multiple_of(m * ROWS, ROWS), ROWS)]
-
-    def hand(self, i):
-        return rc(
-            self.turn,
-            self.rows(self.m),
-            self.send.at[i - 1],
-            self.recv.at[i - 1],
-            (self.s, self.d, (self.m + i) % N),
-        )
-
-    def taken(self, i):
-        ref = self.rows((self.m + N - i) % N)
-        return rc(ref, ref, self.send.at[i - 1], self.recv.at[i - 1], (self.s, self.d, (self.m + i) % N))
-
-    def keep(self):
-        return pltpu.make_async_copy(self.turn, self.rows(self.m), self.local)
+        pl.when(self.d != self.m)(lambda: self.far().start())
+        pl.when(self.d == self.m)(lambda: self.near().start())
 
     def middle(self):
-        pl.when(self.d != self.m)(lambda: self.far.wait_recv())
-        pl.when(self.d == self.m)(lambda: self.near.wait())
-        for i in range(1, N):
-            self.hand(i).start()
-        self.keep().start()
+        pl.when(self.d != self.m)(lambda: self.far().wait_recv())
+        pl.when(self.d == self.m)(lambda: self.near().wait())
+        for c in range(SLICE_CHUNKS):
+            self.gather.stage(c, 0)
+
+    def second(self):
+        for c in range(SLICE_CHUNKS):
+            self.gather.stage(c, 1)
+
+    def third(self):
+        for c in range(SLICE_CHUNKS):
+            self.gather.stage(c, 2)
 
     def close(self):
-        for i in range(1, N):
-            self.taken(i).wait_recv()
-        for i in range(1, N):
-            self.hand(i).wait_send()
-        self.keep().wait()
-        pl.when(self.d != self.m)(lambda: self.far.wait_send())
+        for c in range(SLICE_CHUNKS):
+            self.gather.stage(c, 3)
+        self.gather.close()
+        pl.when(self.d != self.m)(lambda: self.far().wait_send())
 
 
 def piece(ref, m, rows=None):
@@ -207,7 +258,7 @@
 
 def gather_kernel(wt, xa, xb, full, slices, turn, w_send, w_recv, w_loc, t_send, t_recv, t_loc, b_send, b_recv, b_loc):
     s, d, m = coords()
-    greet(mp_peers(s, d, m) + dp_near(s, d, m), (d != m, (s, m, d)))
+    greet(mp_near(s, d, m) + dp_near(s, d, m), (d != m, (s, m, d)))
     gather = DpGather(
         4,
         lambda j: wt.at[j],
@@ -234,10 +285,15 @@
     gather.open()
     slots[0].open()
     pl.when(s == 1)(slots[1].open)
-    gather.middle(0)
     slots[0].middle()
     pl.when(s == 1)(slots[1].middle)
-    for j in range(1, 4):
+    gather.middle(0)
+    slots[0].second()
+    pl.when(s == 1)(slots[1].second)
+    gather.middle(1)
+    slots[0].third()
+    pl.when(s == 1)(slots[1].third)
+    for j in range(2, 4):
         gather.middle(j)
     gather.close()
     slots[0].close()
@@ -262,125 +318,122 @@
             DMA((2,)),
             DMA((2,)),
             DMA((2,)),
-            DMA((2, 7)),
-            DMA((2, 7)),
-            DMA((2,)),
+            DMA((2, SLICE_CHUNKS, 7)),
+            DMA((2, SLICE_CHUNKS, 7)),
+            DMA((2, SLICE_CHUNKS)),
         ],
         compiler_params=pltpu.CompilerParams(collective_id=0, has_side_effects=True),
     )(wt, xa, xb)
 
 
 class Relay:
-    def __init__(self, first, terms, resid, total, recv_buf, own, res, summed, landed, sems):
-        self.first, self.terms, self.resid, self.total = first, terms, resid, total
-        self.recv_buf, self.own, self.res, self.summed, self.landed = recv_buf, own, res, summed, landed
-        self.s_send, self.s_recv, self.h_send, self.h_recv, self.g_send, self.g_recv, self.loc = sems
-        self.s, self.d, self.m = coords()
-        self.partner = (1 - self.s, self.d, self.m)
-
-    def peer(self, i):
-        return (self.s, self.d, (self.m + i) % N)
-
-    def scatter(self, c, i):
-        return rc(
-            piece(self.terms, (self.m + i) % N, c * CH),
-            self.recv_buf.at[i - 1, pl.ds(c * CH, CH)],
-            self.s_send.at[c, i - 1],
-            self.s_recv.at[c, i - 1],
-            self.peer(i),
+    def __init__(self, terms, resid, total, bufs, sems):
+        self.terms, self.resid = terms, resid
+        (self.one, self.direct, self.passed, self.mixed, self.kept, self.cross, self.over, self.summed, self.landed) = bufs
+        self.send, self.recv, g_send, g_recv, g_loc = sems
+        s, d, m = coords()
+        x, y = m // 4, m % 4
+        self.x, self.y, self.m = x, y, m
+        self.up, self.down, self.opp = (y + 1) % 4, (y + 3) % 4, (y + 2) % 4
+        self.to_up, self.to_down = (s, d, x * 4 + self.up), (s, d, x * 4 + self.down)
+        self.to_x = (s, d, (1 - x) * 4 + y)
+        self.partner = (1 - s, d, (1 - x) * 4 + y)
+        self.gather = MpGather(
+            CHUNKS,
+            lambda c: self.landed.at[self.rows(c)],
+            lambda mm, c: piece(total, (mm + 4) % N, c * CH),
+            g_send,
+            g_recv,
+            g_loc,
         )
 
-    def hand(self, c):
-        rows = pl.ds(c * CH, CH)
-        return rc(self.summed.at[rows], self.landed.at[rows], self.h_send.at[c], self.h_recv.at[c], self.partner)
-
-    def spread(self, c, i):
-        return rc(
-            self.landed.at[pl.ds(c * CH, CH)],
-            piece(self.total, self.m, c * CH),
-            self.g_send.at[c, i - 1],
-            self.g_recv.at[c, i - 1],
-            self.peer(i),
-        )
-
-    def taken(self, c, i):
-        ref = piece(self.total, (self.m + N - i) % N, c * CH)
-        return rc(ref, ref, self.g_send.at[c, i - 1], self.g_recv.at[c, i - 1], self.peer(i))
-
-    def keep(self, c):
-        return pltpu.make_async_copy(
-            self.landed.at[pl.ds(c * CH, CH)], piece(self.total, self.m, c * CH), self.loc.at[c]
-        )
-
-    def sender_open(self):
+    def rows(self, c):
+        return pl.ds(c * CH, CH)
+
+    def cp(self, c, kind, src, dst, to):
+        return rc(src, dst, self.send.at[c, kind], self.recv.at[c, kind], to)
+
+    def copy(self, c, kind):
+        rows = self.rows(c)
+        return (
+            lambda: self.cp(c, 0, piece(self.terms, self.opp, c * CH), self.one.at[0, rows], self.to_up),
+            lambda: self.cp(c, 1, piece(self.terms, 4 + self.opp, c * CH), self.one.at[1, rows], self.to_down),
+            lambda: self.cp(c, 2, piece(self.terms, 4 + self.up, c * CH), self.direct.at[1, rows], self.to_up),
+            lambda: self.cp(c, 3, piece(self.terms, self.down, c * CH), self.direct.at[0, rows], self.to_down),
+            lambda: self.cp(c, 4, self.mixed.at[0, rows], self.passed.at[0, rows], self.to_up),
+            lambda: self.cp(c, 5, self.mixed.at[1, rows], self.passed.at[1, rows], self.to_down),
+            lambda: self.cp(c, 6, self.cross.at[rows], self.over.at[rows], self.to_x),
+            lambda: self.cp(c, 7, self.summed.at[rows], self.landed.at[rows], self.partner),
+        )[kind]()
+
+    def mine(self, index, c):
+        return self.terms[pl.ds(c * CH, CH), pl.ds(pl.multiple_of(index * PIECE, PIECE), PIECE)].astype(F32)
+
+    def stage(self, c, number):
+        if not 0 <= c < CHUNKS:
+            return
+        rows = self.rows(c)
+        if number == 0:
+            for kind in range(4):
+                self.copy(c, kind).start()
+        elif number == 1:
+            for side, index in ((0, self.up), (1, 4 + self.down)):
+                self.copy(c, side).wait_recv()
+                value = self.one[side, rows].astype(F32) + self.mine(index, c)
+                self.mixed[side, rows] = value.astype(BF16)
+                self.copy(c, 4 + side).start()
+        elif number == 2:
+            for kind in range(2, 6):
+                self.copy(c, kind).wait_recv()
+            for side in range(2):
+                value = self.direct[side, rows].astype(F32) + self.passed[side, rows].astype(F32)
+                value = value + self.mine(side * 4 + self.y, c)
+
+                @pl.when(self.x == side)
+                def _():
+                    self.kept[rows] = value
+
+                @pl.when(self.x != side)
+                def _():
+                    self.cross[rows] = value.astype(BF16)
+
+            self.copy(c, 6).start()
+        else:
+            self.copy(c, 6).wait_recv()
+            value = self.kept[rows] + self.over[rows].astype(F32)
+            if self.resid is not None:
+                value = value + self.resid[rows].astype(F32)
+            self.summed[rows] = value.astype(BF16)
+            self.copy(c, 7).start()
+
+    def sender(self):
+        for tick in range(CHUNKS + 3):
+            for number in range(4):
+                self.stage(tick - number, number)
         for c in range(CHUNKS):
-            for i in range(1, N):
-                self.scatter(c, i).start()
-        own = pltpu.make_async_copy(piece(self.terms, self.m), self.own, self.loc.at[0])
-        own.start()
-        if self.resid is not None:
-            res = pltpu.make_async_copy(piece(self.resid, self.m), self.res, self.loc.at[1])
-            res.start()
-            res.wait()
-        own.wait()
-
-    def sender_rest(self):
-        for c in range(CHUNKS):
-            rows = pl.ds(c * CH, CH)
-            for i in range(1, N):
-                self.scatter(c, i).wait_recv()
-            acc = self.own[rows].astype(F32)
-            for i in range(1, N):
-                acc = acc + self.recv_buf[i - 1, rows].astype(F32)
-            if self.resid is not None:
-                acc = acc + self.res[rows].astype(F32)
-            self.summed[rows] = acc.astype(BF16)
-            self.hand(c).start()
-        for c in range(CHUNKS):
-            for i in range(1, N):
-                self.scatter(c, i).wait_send()
-            self.hand(c).wait_send()
+            for kind in range(8):
+                self.copy(c, kind).wait_send()
 
     def taker(self):
-        for c in range(CHUNKS):
-            self.hand(c).wait_recv()
-            for i in range(1, N):
-                self.spread(c, i).start()
-            self.keep(c).start()
-        for c in range(CHUNKS):
-            for i in range(1, N):
-                self.taken(c, i).wait_recv()
-            for i in range(1, N):
-                self.spread(c, i).wait_send()
-            self.keep(c).wait()
-
-
-RELAY_SCRATCH = [
-    pltpu.VMEM((7, ROWS, PIECE), BF16),
-    pltpu.VMEM((ROWS, PIECE), BF16),
-    pltpu.VMEM((ROWS, PIECE), BF16),
-    pltpu.VMEM((ROWS, PIECE), BF16),
-    pltpu.VMEM((ROWS, PIECE), BF16),
-    DMA((CHUNKS, 7)),
-    DMA((CHUNKS, 7)),
-    DMA((CHUNKS,)),
-    DMA((CHUNKS,)),
-    DMA((CHUNKS, 7)),
-    DMA((CHUNKS, 7)),
-    DMA((CHUNKS,)),
-]
-
-
-def forward_kernel(terms, resid, total, recv_buf, own, res, summed, landed, *sems):
+        for tick in range(CHUNKS + 3):
+            if tick < CHUNKS:
+                self.copy(tick, 7).wait_recv()
+            for number in range(4):
+                self.gather.stage(tick - number, number)
+        self.gather.close()
+
+
+SIDES = pltpu.VMEM((2, ROWS, PIECE), BF16)
+ONE = pltpu.VMEM((ROWS, PIECE), BF16)
+RELAY_BUFS = [SIDES, SIDES, SIDES, SIDES, pltpu.VMEM((ROWS, PIECE), F32), ONE, ONE, ONE, ONE]
+RELAY_SEMS = [DMA((CHUNKS, 8)), DMA((CHUNKS, 8)), DMA((CHUNKS, 7)), DMA((CHUNKS, 7)), DMA((CHUNKS,))]
+
+
+def forward_kernel(terms, resid, total, *rest):
     s, d, m = coords()
-    greet(mp_peers(s, d, m) + [(1 - s, d, m)])
-    relay = Relay(0, terms, resid, total, recv_buf, own, res, summed, landed, sems)
-
-    @pl.when(s == 0)
-    def _():
-        relay.sender_open()
-        relay.sender_rest()
-
+    greet(mp_near(s, d, m) + [(1 - s, d, (m + 4) % N)])
+    relay = Relay(terms, resid, total, rest[:9], rest[9:])
+    pl.when(s == 0)(relay.sender)
     pl.when(s == 1)(relay.taker)
 
 
@@ -389,18 +442,19 @@
         forward_kernel,
         name="relay_forward",
         out_shape=jax.ShapeDtypeStruct((ROWS, D), BF16),
-        in_specs=[ANY, ANY],
-        out_specs=HBM,
-        scratch_shapes=list(RELAY_SCRATCH),
+        in_specs=[VM, VM],
+        out_specs=VM,
+        scratch_shapes=RELAY_BUFS + RELAY_SEMS,
         compiler_params=pltpu.CompilerParams(collective_id=1, has_side_effects=True),
     )(terms, resid)
 
 
-def backward_kernel(terms, ctx, before, total, rights, recv_buf, own, res, summed, landed, *sems):
+def backward_kernel(terms, ctx, before, total, rights, *rest):
     s, d, m = coords()
-    greet(mp_peers(s, d, m) + dp_near(s, d, m) + [(1 - s, d, m)])
-    relay_sems, (y_send, y_recv, y_loc) = sems[:7], sems[7:]
-    relay = Relay(1, terms, None, total, recv_buf, own, res, summed, landed, relay_sems)
+    greet(mp_near(s, d, m) + dp_near(s, d, m) + [(1 - s, d, (m + 4) % N)])
+    relay = Relay(terms, None, total, rest[:9], rest[9:14])
+    y_send, y_recv, y_loc, over = rest[14:]
+    keep = pltpu.make_async_copy(before, total, over)
     gather = DpGather(
         1,
         lambda j: ctx,
@@ -410,9 +464,14 @@
         y_recv,
         y_loc,
     )
-    pl.when(s == 1)(relay.sender_open)
     gather.open()
-    pl.when(s == 1)(relay.sender_rest)
+
+    @pl.when(s == 1)
+    def _():
+        keep.start()
+        relay.sender()
+        keep.wait()
+
     gather.middle(0)
     gather.close()
     pl.when(s == 0)(relay.taker)
@@ -426,10 +485,9 @@
             jax.ShapeDtypeStruct((ROWS, D), BF16),
             jax.ShapeDtypeStruct((4, N * ROWS, PIECE), BF16),
         ),
-        in_specs=[ANY, VM, HBM],
-        out_specs=(HBM, HBM),
-        scratch_shapes=list(RELAY_SCRATCH) + [DMA((1, 8)), DMA((1, 8)), DMA((1,))],
-        input_output_aliases={2: 0},
+        in_specs=[VM, VM, VM],
+        out_specs=(VM, HBM),
+        scratch_shapes=RELAY_BUFS + RELAY_SEMS + [DMA((1, 8)), DMA((1, 8)), DMA((1,)), DMA],
         compiler_params=pltpu.CompilerParams(collective_id=2, has_side_effects=True),
     )(terms, ctx, before)
 
@@ -483,15 +541,17 @@
     norm_own[...] = acc
     over = rc(norm_own, norm_far, f_send, f_recv, (1 - s, d, m))
     over.start()
+    gather.middle(0)
     slot.middle()
-    gather.middle(0)
     over.wait_recv()
     both = norm_own[...] + norm_far[...]
     norm_dp[...] = both
     norms[d] = both
     for i in range(1, N):
         to_dp(i).start()
+    slot.second()
     gather.middle(1)
+    slot.third()
     gather.middle(2)
     gather.close()
     slot.close()
@@ -527,9 +587,9 @@
             DMA,
             DMA,
             DMA,
-            DMA((7,)),
-            DMA((7,)),
-            DMA,
+            DMA((SLICE_CHUNKS, 7)),
+            DMA((SLICE_CHUNKS, 7)),
+            DMA((SLICE_CHUNKS,)),
             DMA((7,)),
             DMA((7,)),
             DMA,
@@ -746,7 +806,8 @@
         return q, k, v, thin, ctx, back_term(ctx, mats[3]).astype(BF16)
 
     q, k, v, gctx, ctx, terms = lax.cond(is_dec, first_dec, first_enc)
-    relayed = relay_forward(terms, own_inputs)
+    own_piece = lax.dynamic_slice_in_dim(own_inputs, lax.axis_index("mp") * PIECE, PIECE, 1)
+    relayed = relay_forward(terms, own_piece)
 
     def second_dec():
         k, v = project(relayed, mats[1]), project(relayed, mats[2])

time: 335 us -> 319 us (0.952)
  Pallas kernels: 299 us -> 281 us
    pallas_call x1, Pallas kernels: 92.8 us -> 79.9 us  [relay_backward(): pl.pallas_call(backward_kernel, name='relay_backward', out_shape=(jax.Sha...]
    pallas_call x1, Pallas kernels: 56.1 us -> 51.7 us  [gather_grads(): pl.pallas_call(final_kernel, name='gather_grads', out_shape=(jax.ShapeDty...]
where the time goes in v2:
time: 319 us; the launch traced here: 318 us
  Pallas kernels  281 us (88%)
  matrix products  19.9 us (6%)
  other arithmetic  8.37 us (3%)
  local copies, waits for them, and re-layouts  8.3 us (3%)
    pallas_call x1, Pallas kernels, gather_weights(): pl.pallas_call(gather_kernel, name='gather_weights', out_shape=(jax.Shape...  85.9 us
    pallas_call x1, Pallas kernels, relay_backward(): pl.pallas_call(backward_kernel, name='relay_backward', out_shape=(jax.Sha...  79.9 us
    pallas_call x1, Pallas kernels, gather_grads(): pl.pallas_call(final_kernel, name='gather_grads', out_shape=(jax.ShapeDty...  51.7 us
    pallas_call x1, Pallas kernels, relay_forward(): pl.pallas_call(forward_kernel, name='relay_forward', out_shape=jax.ShapeD...  34.7 us
    dot_general x4, matrix products, project(): return jnp.dot(left, right, preferred_element_type=F32).astype(BF16)  15.1 us
    pallas_call x1, Pallas kernels, weight_grads(): pl.pallas_call(weight_kernel, name='weight_grads', grid=(PIECE // BLOCK,)...  13.6 us

profile of v2, /device:TPU:1, one launch (start us, length us, event | category | flops | bytes accessed | tf_op | source)
XLA Modules:
  0.0 318.1 jit_solution(3062045579579884805)
XLA Ops:
  0.6 0.0 copy-start.10
  0.6 0.0 copy-start.4
  0.7 0.9 mul.46
  1.5 2.1 multiply_reduce_fusion
  3.6 0.0 copy-start.5
  3.6 2.4 multiply_convert_fusion.xa
  6.0 0.0 copy-done.10
  6.0 0.1 compare_convert_fusion
  6.1 0.0 copy-done.4
  6.1 1.5 broadcast_multiply_fusion
  7.6 0.0 copy-done.5
  7.6 1.7 copy.13
  9.4 85.9 %gather_weights.1 = (bf16[4,8,512,512]{3,2,1,0:T(8,128)(2,1)}, bf16[3,2048,512]{2,1,0:T(8,128)(2,1)}) custom-call(bf16[4,512,512]{2,1,0:T(8,128)(2,1)} %bitcast.79, bf16[256,4096]{1,0:T(8,128)(2,1)S(1)} %multiply_convert_fusion.xa, bf16[256,4096]{1,0:T(8,128)(2,1)} %bitcast.75), custom_call_target="tpu_custom_call" | custom-call | tf_op jit(solution)/shard_map/gather_weights/pallas_call | solution.py:304
  95.2 18.9 %conditional.4 = (bf16[256,512]{1,0:T(8,128)(2,1)S(1)}, bf16[256,512]{1,0:T(8,128)(2,1)S(1)}, bf16[256,512]{1,0:T(8,128)(2,1)S(1)}, bf16[256,512]{1,0:T(8,128)(2...) conditional(s32[]{:T(128)} %convert_element_type.53, (bf16[4,4096,512]{2,1,0:T(8,128)(2,1)}, ...), branch_computations={%region_1.0_spmd, %region_2.0_spmd} | conditional | flops 4296278016 | bytes 26476594
  95.2 3.4 %fusion.11.k_ref = bf16[256,512]{1,0:T(8,128)(2,1)S(1)} fusion(bf16[256,4096]{1,0:T(8,128)(2,1)S(1)} %get-tuple-element.49, bf16[4,4096,512]{2,1,0:T(8,128)(2,1)} %get-tuple-element.50), kind=kOutput, calls=%fused_computation.12 | convolution fusion | flops 1073872896 | bytes 6553600 | tf_op jit(solution)/shard_map/cond/branch_0_fun/dot_general | solution.py:777
  98.7 3.4 %fusion.14.v_ref = bf16[256,512]{1,0:T(8,128)(2,1)S(1)} fusion(bf16[256,4096]{1,0:T(8,128)(2,1)S(1)} %get-tuple-element.49, bf16[4,4096,512]{2,1,0:T(8,128)(2,1)} %get-tuple-element.50), kind=kOutput, calls=%fused_computation.13 | convolution fusion | flops 1073872896 | bytes 6553600 | tf_op jit(solution)/shard_map/cond/branch_0_fun/dot_general | solution.py:777
  102.1 3.4 %fusion.5.q_ref = bf16[256,512]{1,0:T(8,128)(2,1)S(1)} fusion(bf16[256,4096]{1,0:T(8,128)(2,1)S(1)} %get-tuple-element.49, bf16[4,4096,512]{2,1,0:T(8,128)(2,1)} %get-tuple-element.50), kind=kOutput, calls=%fused_computation.6 | convolution fusion | flops 1073741824 | bytes 6553600 | tf_op jit(solution)/shard_map/cond/branch_0_fun/dot_general | solution.py:777
  105.6 3.8 %attend.1 = bf16[256,512]{1,0:T(8,128)(2,1)S(1)} custom-call(s32[2]{0:T(128)S(1)} %get-tuple-element.51.lens, bf16[256,512]{1,0:T(8,128)(2,1)S(1)} %fusion.5.q_ref, bf16[256,512]{1,0:T(8,128)(2,1)S(1)} %fusion.11.k_ref, bf16[256,512]{1,0:T(8,128)(2,1)S(1)} %fusion.14.v_ref), custom_call_target="tpu_custom_call" | custom-call | tf_op jit(solution)/shard_map/cond/branch_0_fun/attend/pallas_call | solution.py:646
  109.3 4.8 %convolution_convert_fusion = bf16[256,4096]{1,0:T(8,128)(2,1)} fusion(bf16[256,512]{1,0:T(8,128)(2,1)S(1)} %attend.1, bf16[4,4096,512]{2,1,0:T(8,128)(2,1)} %get-tuple-element.50), kind=kOutput, calls=%fused_computation | convolution fusion | flops 1074790400 | bytes 6553600 | tf_op jit(solution)/shard_map/cond/branch_0_fun/sj,dj->sd/dot_general | solution.py:781
  114.2 0.0 copy-start.8
  114.2 0.0 copy-start.6
  114.2 1.9 constant_dynamic-slice_fusion.resid
  116.1 34.7 %relay_forward.1.before = bf16[256,4096]{1,0:T(8,128)(2,1)} custom-call(bf16[256,4096]{1,0:T(8,128)(2,1)} %get-tuple-element.98.terms, bf16[256,512]{1,0:T(8,128)(2,1)} %constant_dynamic-slice_fusion.resid), custom_call_target="tpu_custom_call" | custom-call | tf_op jit(solution)/shard_map/relay_forward/pallas_call | solution.py:441
  150.8 0.0 copy-done.8
  150.8 0.0 copy-done.6
  150.8 3.1 conditional.5
  150.8 1.6 broadcast_in_dim.20
  152.4 0.7 broadcast_in_dim.14.clone
  153.1 0.7 broadcast_in_dim.14.clone.1
  153.9 0.0 copy-start.7
  153.9 0.0 copy-start.9
  153.9 79.9 %relay_backward.1 = (bf16[256,4096]{1,0:T(8,128)(2,1)}, bf16[4,2048,512]{2,1,0:T(8,128)(2,1)}) custom-call(bf16[256,4096]{1,0:T(8,128)(2,1)} %get-tuple-element.101.terms, bf16[256,512]{1,0:T(8,128)(2,1)S(1)} %get-tuple-element.102.ctx, bf16[256,4096]{1,0:T(8,128)(2,1)} %relay_forward.1.before), custom_call_target="tpu_custom_call" | custom-call | tf_op jit(solution)/shard_map/relay_backward/pallas_call | solution.py:481
  233.7 0.0 copy-done.7
  233.7 0.0 copy-done.9
  233.7 11.0 %conditional.6 = ((bf16[256,512]{1,0:T(8,128)(2,1)S(1)}, bf16[256,512]{1,0:T(8,128)(2,1)}, bf16[256,512]{1,0:T(8,128)(2,1)})) conditional(s32[]{:T(128)} %convert_element_type.53, (bf16[4,4096,512]{2,1,0:T(8,128)(2,1)}, bf16[256,4096]{1,0:T(8,128)(2,1)}, s32[2]{0:T(128)S(1)}, bf16[256,512]{1,0:T(8,128)(2,1)S(1)}, bf16[256,512]{1,0:T(8,128)(2,1)S(1)}, ...), branch_computations={%region_5.0_spmd, %region_6.0_spmd} | conditional | flops 1073872896 | bytes 6553632 | solution.py:831
  233.8 4.8 %fusion.47.g_ref = bf16[256,512]{1,0:T(8,128)(2,1)} fusion(bf16[256,4096]{1,0:T(8,128)(2,1)} %get-tuple-element.68, bf16[4,4096,512]{2,1,0:T(8,128)(2,1)} %get-tuple-element.69), kind=kOutput, calls=%fused_computation.39 | convolution fusion | flops 1073872896 | bytes 6553600 | tf_op jit(solution)/shard_map/cond/branch_0_fun/dot_general | solution.py:777
  238.5 6.2 %attend_all.3 = (bf16[256,512]{1,0:T(8,128)(2,1)}, bf16[256,512]{1,0:T(8,128)(2,1)S(1)}, bf16[256,512]{1,0:T(8,128)(2,1)}, bf16[256,512]{1,0:T(8,128)(2,1)}) custom-call(s32[2]{0:T(128)S(1)} %get-tuple-element.64.lens, bf16[256,512]{1,0:T(8,128)(2,1)S(1)} %get-tuple-element.65.q_ref, bf16[256,512]{1,0:T(8,128)(2,1)S(1)} %get-tuple-element.66.k_ref, ...), custom_call_target="tpu_custom_call" | custom-call | tf_op jit(solution)/shard_map/cond/branch_0_fun/attend_all/pallas_call | solution.py:684
  244.7 0.0 copy-start.3
  244.7 5.0 %norm_parts.1.norm = f32[8,128]{1,0:T(8,128)} custom-call(s32[1]{0:T(128)} %bitcast.9.sec, bf16[256,4096]{1,0:T(8,128)(2,1)S(1)} %multiply_convert_fusion.xa, bf16[256,4096]{1,0:T(8,128)(2,1)} %bitcast.77, bf16[256,4096]{1,0:T(8,128)(2,1)} %get-tuple-element.103.xr.relayed, bf16[256,512]{1,0:T(8,128)(2,1)S(1)} %get-tuple-element.109.gq, ...), custom_call_target="tpu_custom_call" | custom-call | tf_op jit(solution)/shard_map/norm_parts/pallas_call | solution.py:721
  249.8 0.0 copy-done.3
  249.8 51.7 %gather_grads.1 = (bf16[3,2048,512]{2,1,0:T(8,128)(2,1)}, bf16[4,2048,512]{2,1,0:T(8,128)(2,1)}, f32[8,8,128]{2,1,0:T(8,128)}) custom-call(bf16[256,512]{1,0:T(8,128)(2,1)S(1)} %get-tuple-element.109.gq, bf16[256,512]{1,0:T(8,128)(2,1)S(1)} %copy-done.3, bf16[256,512]{1,0:T(8,128)(2,1)} %get-tuple-element.111.gv, ...), custom_call_target="tpu_custom_call", output_to_operand_aliasing={{0}: (5, {}), {1}: (6, {})} | custom-call | tf_op jit(solution)/shard_map/gather_grads/pallas_call | solution.py:568
  301.5 0.5 broadcast.51
  302.0 1.4 fusion.50
  303.5 0.6 div.17.clip
  304.1 13.6 %weight_grads.1 = f32[512,4,512]{2,1,0:T(4,128)} custom-call(s32[1]{0:T(128)} %bitcast.9.sec, f32[16]{0:T(128)} %div.17.clip, bf16[3,2048,512]{2,1,0:T(8,128)(2,1)} %get-tuple-element.115.x_ref, bf16[4,2048,512]{2,1,0:T(8,128)(2,1)} %get-tuple-element.116.y_ref, f32[512,4,512]{2,1,0:T(4,128)} %bitcast.84), custom_call_target="tpu_custom_call" | custom-call | tf_op jit(solution)/shard_map/weight_grads/pallas_call | solution.py:753
  317.6 0.5 dynamic-slice_bitcast_fusion
  (4 shorter events, 0.1 us)
Async XLA Ops:
  0.6 5.4 %copy-start.10 = (s32[2,2]{1,0:T(2,128)S(1)}, s32[2,2]{1,0:T(2,128)}, u32[]{:S(2)}) copy-start(s32[2,2]{1,0:T(2,128)} %param.16) | copy-start | bytes 52
  0.6 5.5 %copy-start.4 = (bf16[2,128,4096]{2,1,0:T(8,128)(2,1)S(1)}, bf16[2,128,4096]{2,1,0:T(8,128)(2,1)}, u32[]{:S(2)}) copy-start(bf16[2,128,4096]{2,1,0:T(8,128)(2,1)} %param.15) | copy-start | bytes 6291460
  3.6 4.0 %copy-start.5 = (bf16[1,512,4,512]{3,2,1,0:T(4,128)(2,1)S(1)}, bf16[1,512,4,512]{3,2,1,0:T(4,128)(2,1)}, u32[]{:S(2)}) copy-start(bf16[1,512,4,512]{3,2,1,0:T(4,128)(2,1)} %param.14) | copy-start | bytes 6291460
  114.2 36.6 %copy-start.8 = (bf16[256,512]{1,0:T(8,128)(2,1)}, bf16[256,512]{1,0:T(8,128)(2,1)S(1)}, u32[]{:S(2)}) copy-start(bf16[256,512]{1,0:T(8,128)(2,1)S(1)} %get-tuple-element.105) | copy-start | bytes 786436
  114.2 36.6 %copy-start.6 = (bf16[256,512]{1,0:T(8,128)(2,1)}, bf16[256,512]{1,0:T(8,128)(2,1)S(1)}, u32[]{:S(2)}) copy-start(bf16[256,512]{1,0:T(8,128)(2,1)S(1)} %get-tuple-element.104) | copy-start | bytes 786436
  153.9 79.9 %copy-start.7 = (bf16[256,512]{1,0:T(8,128)(2,1)S(1)}, bf16[256,512]{1,0:T(8,128)(2,1)}, u32[]{:S(2)}) copy-start(bf16[256,512]{1,0:T(8,128)(2,1)} %copy-done.6) | copy-start | bytes 786436
  153.9 79.9 %copy-start.9 = (bf16[256,512]{1,0:T(8,128)(2,1)S(1)}, bf16[256,512]{1,0:T(8,128)(2,1)}, u32[]{:S(2)}) copy-start(bf16[256,512]{1,0:T(8,128)(2,1)} %copy-done.8) | copy-start | bytes 786436
  244.7 5.0 %copy-start.3 = (bf16[256,512]{1,0:T(8,128)(2,1)S(1)}, bf16[256,512]{1,0:T(8,128)(2,1)}, u32[]{:S(2)}) copy-start(bf16[256,512]{1,0:T(8,128)(2,1)} %get-tuple-element.110.gk) | copy-start | bytes 786436

commit v3 on v2

--- a/solution.py
+++ b/solution.py
@@ -16,7 +16,7 @@
 N = 8
 ROWS = 256
 PIECE = 512
-CHUNKS = 4
+CHUNKS = 8
 CH = ROWS // CHUNKS
 ANY = pl.BlockSpec(memory_space=pl.ANY)
 HBM = pl.BlockSpec(memory_space=pltpu.HBM)
@@ -192,12 +192,13 @@
             self.out(c, kind).start()
         if number == 0:
             self.keep(c).start()
+        if number == 3:
+            self.keep(c).wait()
 
     def close(self):
         for c in range(self.chunks):
             for kind in range(7):
                 self.out(c, kind).wait_send()
-            self.keep(c).wait()
 
 
 def mp_near(s, d, m):
@@ -373,15 +374,14 @@
         if not 0 <= c < CHUNKS:
             return
         rows = self.rows(c)
-        if number == 0:
-            for kind in range(4):
-                self.copy(c, kind).start()
-        elif number == 1:
+        if number == 1:
             for side, index in ((0, self.up), (1, 4 + self.down)):
                 self.copy(c, side).wait_recv()
                 value = self.one[side, rows].astype(F32) + self.mine(index, c)
                 self.mixed[side, rows] = value.astype(BF16)
                 self.copy(c, 4 + side).start()
+            for kind in (2, 3):
+                self.copy(c, kind).start()
         elif number == 2:
             for kind in range(2, 6):
                 self.copy(c, kind).wait_recv()
@@ -401,15 +401,23 @@
         else:
             self.copy(c, 6).wait_recv()
             value = self.kept[rows] + self.over[rows].astype(F32)
-            if self.resid is not None:
+            if self.with_resid:
                 value = value + self.resid[rows].astype(F32)
             self.summed[rows] = value.astype(BF16)
             self.copy(c, 7).start()
 
-    def sender(self):
-        for tick in range(CHUNKS + 3):
-            for number in range(4):
-                self.stage(tick - number, number)
+    def sender_open(self):
+        for c in range(CHUNKS):
+            for kind in range(2):
+                self.copy(c, kind).start()
+
+    def sender(self, with_resid):
+        self.with_resid = with_resid
+        for tick in range(CHUNKS + 2):
+            for number in range(1, 4):
+                self.stage(tick + 1 - number, number)
+
+    def sender_close(self):
         for c in range(CHUNKS):
             for kind in range(8):
                 self.copy(c, kind).wait_send()
@@ -420,7 +428,6 @@
                 self.copy(tick, 7).wait_recv()
             for number in range(4):
                 self.gather.stage(tick - number, number)
-        self.gather.close()
 
 
 SIDES = pltpu.VMEM((2, ROWS, PIECE), BF16)
@@ -429,67 +436,170 @@
 RELAY_SEMS = [DMA((CHUNKS, 8)), DMA((CHUNKS, 8)), DMA((CHUNKS, 7)), DMA((CHUNKS, 7)), DMA((CHUNKS,))]
 
 
-def forward_kernel(terms, resid, total, *rest):
-    s, d, m = coords()
-    greet(mp_near(s, d, m) + [(1 - s, d, (m + 4) % N)])
-    relay = Relay(terms, resid, total, rest[:9], rest[9:])
-    pl.when(s == 0)(relay.sender)
-    pl.when(s == 1)(relay.taker)
-
-
-def relay_forward(terms, resid):
-    return pl.pallas_call(
-        forward_kernel,
-        name="relay_forward",
-        out_shape=jax.ShapeDtypeStruct((ROWS, D), BF16),
-        in_specs=[VM, VM],
-        out_specs=VM,
-        scratch_shapes=RELAY_BUFS + RELAY_SEMS,
-        compiler_params=pltpu.CompilerParams(collective_id=1, has_side_effects=True),
-    )(terms, resid)
-
-
-def backward_kernel(terms, ctx, before, total, rights, *rest):
+def bridge_kernel(
+    lens, q_ref, k_in, v_in, g_in, resid, xa, xb, mats, ctx_ref, gq_ref, gk_ref, gv_ref, total, norm, rights, *rest
+):
     s, d, m = coords()
     greet(mp_near(s, d, m) + dp_near(s, d, m) + [(1 - s, d, (m + 4) % N)])
-    relay = Relay(terms, None, total, rest[:9], rest[9:14])
-    y_send, y_recv, y_loc, over = rest[14:]
-    keep = pltpu.make_async_copy(before, total, over)
+    bufs, sems = rest[:9], rest[9:14]
+    y_send, y_recv, y_loc, w_sem, wbuf, terms, k_mid, v_mid, g_mid, gram_a, gram_b = rest[14:]
+    relay = Relay(terms, resid, total, bufs, sems)
     gather = DpGather(
         1,
-        lambda j: ctx,
+        lambda j: ctx_ref,
         lambda j, b: rights.at[3, pl.ds(pl.multiple_of(b * ROWS, ROWS), ROWS)],
         lambda j, b, h: rights.at[3, pl.ds(pl.multiple_of(b * ROWS + h * 128, 128), 128)],
         y_send,
         y_recv,
         y_loc,
     )
-    gather.open()
+
+    def load(mat, slot):
+        return pltpu.make_async_copy(mats.at[mat], wbuf.at[slot], w_sem.at[slot])
+
+    def block(slot, index):
+        return wbuf[slot, pl.ds(pl.multiple_of(index * PIECE, PIECE), PIECE)]
+
+    def put(index, value):
+        terms[:, pl.ds(pl.multiple_of(index * PIECE, PIECE), PIECE)] = value.astype(BF16)
+
+    def send_terms(term):
+        for group in ((relay.opp, 4 + relay.opp), (relay.up, 4 + relay.down, 4 + relay.up, relay.down)):
+            for index in group:
+                put(index, term(index))
+            if group[0] is relay.opp:
+                relay.sender_open()
+        for index in (relay.y, 4 + relay.y):
+            put(index, term(index))
+
+    def grams(src, dst):
+        for e in range(2):
+            rows = src[pl.ds(e * 128, 128)]
+            dst[e] = dot_nt(rows, rows)
+
+    def thin_gram(ref, e):
+        rows = ref[pl.ds(e * 128, 128)]
+        return dot_nt(rows, rows)
+
+    def note(value_of):
+        lane = lax.broadcasted_iota(jnp.int32, (8, 128), 1)
+        norm[...] = jnp.where(lane == 0, jnp.sum(value_of(0)), 0.0) + jnp.where(lane == 1, jnp.sum(value_of(1)), 0.0)
+
+    def wide_dot(left, slot, out):
+        for half in range(2):
+            cols = slice(half * 256, half * 256 + 256)
+            out[:, cols] = dot_nn(left[...], wbuf[slot, :, cols]).astype(BF16)
+
+    def each_head(body):
+        @pl.loop(0, 2)
+        def _(e):
+            rows = pl.ds(pl.multiple_of(e * 128, 128), 128)
+            key_ok = lax.broadcasted_iota(jnp.int32, (128, 128), 1) < lens[e]
+            for pair in range(4):
+                body(rows, slice(pair * 128, pair * 128 + 128), key_ok)
+
+    @pl.when(s == 0)
+    def _():
+        load(3, 0).start()
+
+        def ahead(rows, cols, key_ok):
+            ctx_ref[rows, cols] = context(q_ref[rows, cols], k_in[rows, cols], v_in[rows, cols], key_ok)
+
+        each_head(ahead)
+        gather.open()
+        load(3, 0).wait()
+        send_terms(lambda index: dot_nt(ctx_ref[...], block(0, index)))
+        relay.sender(True)
+        gather.middle(0)
+        grams(xa, gram_a)
+        gather.close()
+        relay.taker()
+        wide_dot(total, 0, g_mid)
+
+        def back(rows, cols, key_ok):
+            _, gq, gk, gv = gradients(
+                q_ref[rows, cols], k_in[rows, cols], v_in[rows, cols], g_mid[rows, cols], key_ok, False
+            )
+            gq_ref[rows, cols], gk_ref[rows, cols], gv_ref[rows, cols] = gq, gk, gv
+
+        each_head(back)
+        grams(total, gram_b)
+        note(
+            lambda e: gram_a[e] * (thin_gram(gq_ref, e) + thin_gram(gk_ref, e) + thin_gram(gv_ref, e))
+            + gram_b[e] * thin_gram(ctx_ref, e)
+        )
+        relay.sender_close()
+        relay.gather.close()
 
     @pl.when(s == 1)
     def _():
-        keep.start()
-        relay.sender()
-        keep.wait()
-
-    gather.middle(0)
-    gather.close()
-    pl.when(s == 0)(relay.taker)
-
-
-def relay_backward(terms, ctx, before):
+        load(1, 0).start()
+        load(2, 1).start()
+        grams(xa, gram_a)
+        grams(xb, gram_b)
+        load(1, 0).wait()
+        load(2, 1).wait()
+        relay.taker()
+        wide_dot(total, 0, k_mid)
+        wide_dot(total, 1, v_mid)
+
+        def both(rows, cols, key_ok):
+            ctx, gq, gk, gv = gradients(
+                q_ref[rows, cols], k_mid[rows, cols], v_mid[rows, cols], g_in[rows, cols], key_ok, True
+            )
+            ctx_ref[rows, cols], gq_ref[rows, cols], gk_ref[rows, cols], gv_ref[rows, cols] = ctx, gq, gk, gv
+
+        each_head(both)
+        send_terms(lambda index: dot_nt(gk_ref[...], block(0, index)) + dot_nt(gv_ref[...], block(1, index)))
+        gather.open()
+        relay.sender(False)
+        gather.middle(0)
+
+        def value_of(e):
+            rows = total[pl.ds(e * 128, 128)]
+            return (
+                gram_a[e] * thin_gram(gq_ref, e)
+                + dot_nt(rows, rows) * (thin_gram(gk_ref, e) + thin_gram(gv_ref, e))
+                + gram_b[e] * thin_gram(ctx_ref, e)
+            )
+
+        note(value_of)
+        gather.close()
+        relay.sender_close()
+        relay.gather.close()
+
+
+def bridge(lens, q, k, v, g, resid, xa, xb, mats):
+    thin = jax.ShapeDtypeStruct((ROWS, PIECE), BF16)
+    small = pltpu.VMEM((ROWS, PIECE), BF16)
     return pl.pallas_call(
-        backward_kernel,
-        name="relay_backward",
-        out_shape=(
+        bridge_kernel,
+        name="bridge",
+        out_shape=(thin,) * 4
+        + (
             jax.ShapeDtypeStruct((ROWS, D), BF16),
+            jax.ShapeDtypeStruct((8, 128), F32),
             jax.ShapeDtypeStruct((4, N * ROWS, PIECE), BF16),
         ),
-        in_specs=[VM, VM, VM],
-        out_specs=(VM, HBM),
-        scratch_shapes=RELAY_BUFS + RELAY_SEMS + [DMA((1, 8)), DMA((1, 8)), DMA((1,)), DMA],
-        compiler_params=pltpu.CompilerParams(collective_id=2, has_side_effects=True),
-    )(terms, ctx, before)
+        in_specs=[SM] + [VM] * 7 + [HBM],
+        out_specs=(VM,) * 6 + (HBM,),
+        scratch_shapes=RELAY_BUFS
+        + RELAY_SEMS
+        + [
+            DMA((1, 8)),
+            DMA((1, 8)),
+            DMA((1,)),
+            DMA((2,)),
+            pltpu.VMEM((2, D, PIECE), BF16),
+            pltpu.VMEM((ROWS, D), BF16),
+            small,
+            small,
+            small,
+            pltpu.VMEM((2, 128, 128), F32),
+            pltpu.VMEM((2, 128, 128), F32),
+        ],
+        compiler_params=pltpu.CompilerParams(collective_id=1, has_side_effects=True),
+    )(lens, q, k, v, g, resid, xa, xb, mats)
 
 
 def final_kernel(
@@ -528,9 +638,9 @@
         ref = norms.at[(d + N - i) % N]
         return rc(ref, ref, e_send.at[i - 1], e_recv.at[i - 1], (s, (d + i) % N, m))
 
+    slot.open()
     for i in range(1, N):
         to_mp(i).start()
-    slot.open()
     gather.open()
     norm_mp[m] = norm[...]
     for i in range(1, N):
@@ -541,17 +651,17 @@
     norm_own[...] = acc
     over = rc(norm_own, norm_far, f_send, f_recv, (1 - s, d, m))
     over.start()
+    slot.middle()
     gather.middle(0)
-    slot.middle()
+    slot.second()
     over.wait_recv()
     both = norm_own[...] + norm_far[...]
     norm_dp[...] = both
     norms[d] = both
     for i in range(1, N):
         to_dp(i).start()
-    slot.second()
+    slot.third()
     gather.middle(1)
-    slot.third()
     gather.middle(2)
     gather.close()
     slot.close()
@@ -627,105 +737,31 @@
     return weights / jnp.sum(weights, axis=-1, keepdims=True)
 
 
-def attend_kernel(lens, q_ref, k_ref, v_ref, ctx_ref):
-    key_ok = lax.broadcasted_iota(jnp.int32, (128, 128), 1) < lens[pl.program_id(0)]
-    masks = head_masks()
-    for pair in range(4):
-        cols = slice(pair * 128, pair * 128 + 128)
-        q, k, v = q_ref[:, cols], k_ref[:, cols], v_ref[:, cols]
-        zero = jnp.zeros_like(q)
-        ctx = jnp.zeros((128, 128), F32)
-        for mask in masks:
-            probs = soft(q, k, mask, key_ok)
-            ctx = ctx + dot_nn(probs.astype(BF16), jnp.where(mask, v, zero))
-        ctx_ref[:, cols] = ctx.astype(BF16)
-
-
-def attend(lens, q, k, v):
-    spec = pl.BlockSpec((128, PIECE), lambda e: (e, 0))
-    return pl.pallas_call(
-        attend_kernel,
-        name="attend",
-        grid=(2,),
-        in_specs=[SM] + [spec] * 3,
-        out_specs=spec,
-        out_shape=jax.ShapeDtypeStruct((ROWS, PIECE), BF16),
-    )(lens, q, k, v)
-
-
-def attend_all_kernel(lens, q_ref, k_ref, v_ref, g_ref, ctx_ref, gq_ref, gk_ref, gv_ref):
-    key_ok = lax.broadcasted_iota(jnp.int32, (128, 128), 1) < lens[pl.program_id(0)]
-    masks = head_masks()
-    for pair in range(4):
-        cols = slice(pair * 128, pair * 128 + 128)
-        q, k, v, g = q_ref[:, cols], k_ref[:, cols], v_ref[:, cols], g_ref[:, cols]
-        zero = jnp.zeros_like(q)
-        ctx = gq = gk = gv = jnp.zeros((128, 128), F32)
-        for mask in masks:
-            probs = soft(q, k, mask, key_ok)
-            low = probs.astype(BF16)
-            g_one = jnp.where(mask, g, zero)
-            gp = dot_nt(g_one, v)
-            inner = jnp.sum(gp * probs, axis=-1, keepdims=True)
-            gs = (probs * (gp - inner) * HEAD ** (-0.5)).astype(BF16)
+def context(q, k, v, key_ok):
+    zero = jnp.zeros_like(q)
+    ctx = jnp.zeros((128, 128), F32)
+    for mask in head_masks():
+        probs = soft(q, k, mask, key_ok)
+        ctx = ctx + dot_nn(probs.astype(BF16), jnp.where(mask, v, zero))
+    return ctx.astype(BF16)
+
+
+def gradients(q, k, v, g, key_ok, with_context):
+    zero = jnp.zeros_like(q)
+    ctx = gq = gk = gv = jnp.zeros((128, 128), F32)
+    for mask in head_masks():
+        probs = soft(q, k, mask, key_ok)
+        low = probs.astype(BF16)
+        g_one = jnp.where(mask, g, zero)
+        gp = dot_nt(g_one, v)
+        inner = jnp.sum(gp * probs, axis=-1, keepdims=True)
+        gs = (probs * (gp - inner) * HEAD ** (-0.5)).astype(BF16)
+        if with_context:
             ctx = ctx + dot_nn(low, jnp.where(mask, v, zero))
-            gq = gq + dot_nn(gs, jnp.where(mask, k, zero))
-            gk = gk + dot_tn(gs, jnp.where(mask, q, zero))
-            gv = gv + dot_tn(low, g_one)
-        ctx_ref[:, cols] = ctx.astype(BF16)
-        gq_ref[:, cols] = gq.astype(BF16)
-        gk_ref[:, cols] = gk.astype(BF16)
-        gv_ref[:, cols] = gv.astype(BF16)
-
-
-def attend_all(lens, q, k, v, g):
-    spec = pl.BlockSpec((128, PIECE), lambda e: (e, 0))
-    shape = jax.ShapeDtypeStruct((ROWS, PIECE), BF16)
-    return pl.pallas_call(
-        attend_all_kernel,
-        name="attend_all",
-        grid=(2,),
-        in_specs=[SM] + [spec] * 4,
-        out_specs=(spec,) * 4,
-        out_shape=(shape,) * 4,
-    )(lens, q, k, v, g)
-
-
-def norm_kernel(sec, xa, xb, xr, gq, gk, gv, ctx, out):
-    example = pl.program_id(0)
-    is_dec = sec[0] == 1
-
-    def gram(ref):
-        return dot_nt(ref[...], ref[...])
-
-    kv, cc = gram(gk) + gram(gv), gram(ctx)
-    none = jnp.zeros_like(cc)
-    total = gram(xa) * (gram(gq) + jnp.where(is_dec, none, kv))
-    total = total + gram(xr) * jnp.where(is_dec, kv, cc) + gram(xb) * jnp.where(is_dec, cc, none)
-    value = jnp.sum(total)
-    lane = lax.broadcasted_iota(jnp.int32, (8, 128), 1)
-    mine = jnp.where(lane == example, value, 0.0)
-
-    @pl.when(example == 0)
-    def _():
-        out[...] = mine
-
-    @pl.when(example == 1)
-    def _():
-        out[...] += mine
-
-
-def norm_parts(sec, xa, xb, xr, gq, gk, gv, ctx):
-    wide = pl.BlockSpec((128, D), lambda e: (e, 0))
-    thin = pl.BlockSpec((128, PIECE), lambda e: (e, 0))
-    return pl.pallas_call(
-        norm_kernel,
-        name="norm_parts",
-        grid=(2,),
-        in_specs=[SM] + [wide] * 3 + [thin] * 4,
-        out_specs=pl.BlockSpec((8, 128), lambda e: (0, 0)),
-        out_shape=jax.ShapeDtypeStruct((8, 128), F32),
-    )(sec, xa, xb, xr, gq, gk, gv, ctx)
+        gq = gq + dot_nn(gs, jnp.where(mask, k, zero))
+        gk = gk + dot_tn(gs, jnp.where(mask, q, zero))
+        gv = gv + dot_tn(low, g_one)
+    return tuple(value.astype(BF16) for value in (ctx, gq, gk, gv))
 
 
 BLOCK = 128
@@ -777,10 +813,6 @@
     return jnp.dot(left, right, preferred_element_type=F32).astype(BF16)
 
 
-def back_term(left, right):
-    return jnp.einsum("sj,dj->sd", left, right, preferred_element_type=F32)
-
-
 def per_device(inputs, norm_gains, weights, cotangent, lengths, dp_noise):
     section = lax.axis_index("section")
     is_dec = section == 1
@@ -795,41 +827,17 @@
     mats = full.reshape(4, D, PIECE)
     lens = lengths[0]
     thin = jnp.zeros((ROWS, PIECE), BF16)
-    wide = jnp.zeros((ROWS, D), BF16)
 
     def first_dec():
-        return project(normed, mats[0]), thin, thin, project(gout, mats[3]), thin, wide
+        return project(normed, mats[0]), thin, thin, project(gout, mats[3])
 
     def first_enc():
         q, k, v = (project(normed, mats[i]) for i in range(3))
-        ctx = attend(lens, q, k, v)
-        return q, k, v, thin, ctx, back_term(ctx, mats[3]).astype(BF16)
-
-    q, k, v, gctx, ctx, terms = lax.cond(is_dec, first_dec, first_enc)
+        return q, k, v, thin
+
+    q, k, v, gctx = lax.cond(is_dec, first_dec, first_enc)
     own_piece = lax.dynamic_slice_in_dim(own_inputs, lax.axis_index("mp") * PIECE, PIECE, 1)
-    relayed = relay_forward(terms, own_piece)
-
-    def second_dec():
-        k, v = project(relayed, mats[1]), project(relayed, mats[2])
-        ctx, gq, gk, gv = attend_all(lens, q, k, v, gctx)
-        terms = (back_term(gk, mats[1]) + back_term(gv, mats[2])).astype(BF16)
-        return ctx, gq, gk, gv, terms
-
-    def second_enc():
-        return ctx, thin, thin, thin, wide
-
-    ctx, gq, gk, gv, terms = lax.cond(is_dec, second_dec, second_enc)
-    relayed, rights = relay_backward(terms, ctx, relayed)
-
-    def third_dec():
-        return gq, gk, gv
-
-    def third_enc():
-        _, gq, gk, gv = attend_all(lens, q, k, v, project(relayed, mats[3]))
-        return gq, gk, gv
-
-    gq, gk, gv = lax.cond(is_dec, third_dec, third_enc)
-    norm = norm_parts(sec, normed, gout, relayed, gq, gk, gv, ctx)
+    ctx, gq, gk, gv, relayed, norm, rights = bridge(lens, q, k, v, gctx, own_piece, normed, gout, mats)
     slices, rights, norms = gather_grads(gq, gk, gv, relayed, norm, slices, rights)
     sq_norm = norms[:, 0, :2]
     bound = jnp.sqrt(jnp.float32(8.0 * D * HEADS * HEAD))

time: 319 us -> 296 us (0.928)
  Pallas kernels: 281 us -> 270 us
  matrix products: 19.9 us -> 10.3 us
    pallas_call x5 -> x1, Pallas kernels: 130 us -> 109 us  [bridge(): pl.pallas_call(bridge_kernel, name='bridge', out_shape=(thin,) * 4 + (jax...]
    pallas_call x1, Pallas kernels: 51.7 us -> 61.7 us  [gather_grads(): pl.pallas_call(final_kernel, name='gather_grads', out_shape=(jax.ShapeDty...]
    dot_general x1 -> x0, matrix products: 4.8 us -> none  [back_term(): return jnp.einsum('sj,dj->sd', left, right, preferred_element_type=F32)]
    dot_general x4 -> x3, matrix products: 15.1 us -> 10.3 us  [project(): return jnp.dot(left, right, preferred_element_type=F32).astype(BF16)]
where the time goes in v3:
time: 296 us; the launch traced here: 295 us
  Pallas kernels  270 us (91%)
  matrix products  10.3 us (3%)
  other arithmetic  8.4 us (3%)
  local copies, waits for them, and re-layouts  5.65 us (2%)
    pallas_call x1, Pallas kernels, bridge(): pl.pallas_call(bridge_kernel, name='bridge', out_shape=(thin,) * 4 + (jax...  109 us
    pallas_call x1, Pallas kernels, gather_weights(): pl.pallas_call(gather_kernel, name='gather_weights', out_shape=(jax.Shape...  85.9 us
    pallas_call x1, Pallas kernels, gather_grads(): pl.pallas_call(final_kernel, name='gather_grads', out_shape=(jax.ShapeDty...  61.7 us
    pallas_call x1, Pallas kernels, weight_grads(): pl.pallas_call(weight_kernel, name='weight_grads', grid=(PIECE // BLOCK,)...  13.6 us
    dot_general x3, matrix products, project(): return jnp.dot(left, right, preferred_element_type=F32).astype(BF16)  10.3 us

profile of v3, /device:TPU:1, one launch (start us, length us, event | category | flops | bytes accessed | tf_op | source)
XLA Modules:
  0.0 295.3 jit_solution(2098746495752235002)
XLA Ops:
  0.6 0.0 copy-start.3
  0.6 0.0 copy-start.1
  0.7 0.9 mul.46
  1.5 2.1 multiply_reduce_fusion
  3.6 0.0 copy-start.2
  3.6 2.4 multiply_convert_fusion.xa
  6.0 0.0 copy-done.3
  6.0 0.5 slice_bitcast_fusion
  6.6 0.1 compare_convert_fusion
  6.6 0.0 copy-done.1
  6.6 1.5 broadcast_multiply_fusion
  8.2 0.0 copy-done.2
  8.2 1.7 copy.13
  9.9 85.9 %gather_weights.1 = (bf16[4,8,512,512]{3,2,1,0:T(8,128)(2,1)}, bf16[3,2048,512]{2,1,0:T(8,128)(2,1)}) custom-call(bf16[4,512,512]{2,1,0:T(8,128)(2,1)} %bitcast.54, bf16[256,4096]{1,0:T(8,128)(2,1)S(1)} %multiply_convert_fusion.xa, bf16[256,4096]{1,0:T(8,128)(2,1)} %bitcast.47), custom_call_target="tpu_custom_call" | custom-call | tf_op jit(solution)/shard_map/gather_weights/pallas_call | solution.py:305
  95.8 10.3 %conditional.2 = (bf16[256,512]{1,0:T(8,128)(2,1)S(1)}, bf16[256,512]{1,0:T(8,128)(2,1)S(1)}, bf16[256,512]{1,0:T(8,128)(2,1)S(1)}, bf16[256,512]{1,0:T(8,128)(2,1)S(1)}) conditional(s32[]{:T(128)} %convert_element_type.35, (bf16[4,4096,512]{2,1,0:T(8,128)(2,1)}, bf16[256,4096]{1,0:T(8,128)(2,1)S(1)}) %tuple.27, (bf16[4,4096,512]{2,1,0:T(8,128)(2,1)}, ...), branch_computations={%region_1.0_spmd, %region_2.0_spmd} | conditional | flops 3221487616 | bytes 22020160
  95.8 3.4 %fusion.12 = bf16[256,512]{1,0:T(8,128)(2,1)S(1)} fusion(bf16[256,4096]{1,0:T(8,128)(2,1)S(1)} %get-tuple-element.15, bf16[4,4096,512]{2,1,0:T(8,128)(2,1)} %get-tuple-element.16), kind=kOutput, calls=%fused_computation.10 | convolution fusion | flops 1073872896 | bytes 6553600 | tf_op jit(solution)/shard_map/cond/branch_0_fun/dot_general | solution.py:813
  99.2 3.4 %fusion.4 = bf16[256,512]{1,0:T(8,128)(2,1)S(1)} fusion(bf16[256,4096]{1,0:T(8,128)(2,1)S(1)} %get-tuple-element.15, bf16[4,4096,512]{2,1,0:T(8,128)(2,1)} %get-tuple-element.16), kind=kOutput, calls=%fused_computation.4 | convolution fusion | flops 1073741824 | bytes 6553600 | tf_op jit(solution)/shard_map/cond/branch_0_fun/dot_general | solution.py:813
  102.7 3.4 %fusion.9 = bf16[256,512]{1,0:T(8,128)(2,1)S(1)} fusion(bf16[256,4096]{1,0:T(8,128)(2,1)S(1)} %get-tuple-element.15, bf16[4,4096,512]{2,1,0:T(8,128)(2,1)} %get-tuple-element.16), kind=kOutput, calls=%fused_computation.9 | convolution fusion | flops 1073872896 | bytes 6553600 | tf_op jit(solution)/shard_map/cond/branch_0_fun/dot_general | solution.py:813
  106.1 1.7 constant_dynamic-slice_fusion.resid
  107.8 109.0 %bridge.1 = (bf16[256,512]{1,0:T(8,128)(2,1)}, bf16[256,512]{1,0:T(8,128)(2,1)}, bf16[256,512]{1,0:T(8,128)(2,1)}, bf16[256,512]{1,0:T(8,128)(2,1)}, bf16[256,40...) custom-call(s32[2]{0:T(128)} %get-tuple-element.55.lens, ...), custom_call_target="tpu_custom_call" | custom-call | tf_op jit(solution)/shard_map/bridge/pallas_call | solution.py:575
  216.9 61.7 %gather_grads.1 = (bf16[3,2048,512]{2,1,0:T(8,128)(2,1)}, bf16[4,2048,512]{2,1,0:T(8,128)(2,1)}, f32[8,8,128]{2,1,0:T(8,128)}) custom-call(bf16[256,512]{1,0:T(8,128)(2,1)} %get-tuple-element.42.gq, bf16[256,512]{1,0:T(8,128)(2,1)} %get-tuple-element.43.gk, bf16[256,512]{1,0:T(8,128)(2,1)} %get-tuple-element.44.gv, ...), custom_call_target="tpu_custom_call", output_to_operand_aliasing={{0}: (5, {}), {1}: (6, {})} | custom-call | tf_op jit(solution)/shard_map/gather_grads/pallas_call | solution.py:678
  278.6 0.5 broadcast.51
  279.1 1.4 fusion.24
  280.5 0.7 div.17.clip
  281.2 13.6 %weight_grads.1 = f32[512,4,512]{2,1,0:T(4,128)} custom-call(s32[1]{0:T(128)} %bitcast.5.sec, f32[16]{0:T(128)} %div.17.clip, bf16[3,2048,512]{2,1,0:T(8,128)(2,1)} %get-tuple-element.50.x_ref, bf16[4,2048,512]{2,1,0:T(8,128)(2,1)} %get-tuple-element.51.y_ref, f32[512,4,512]{2,1,0:T(4,128)} %bitcast.55), custom_call_target="tpu_custom_call" | custom-call | tf_op jit(solution)/shard_map/weight_grads/pallas_call | solution.py:789
  294.8 0.5 dynamic-slice_bitcast_fusion
  (2 shorter events, 0.0 us)
Async XLA Ops:
  0.6 5.4 %copy-start.3 = (s32[2,2]{1,0:T(2,128)S(1)}, s32[2,2]{1,0:T(2,128)}, u32[]{:S(2)}) copy-start(s32[2,2]{1,0:T(2,128)} %param.12) | copy-start | bytes 52
  0.6 6.0 %copy-start.1 = (bf16[2,128,4096]{2,1,0:T(8,128)(2,1)S(1)}, bf16[2,128,4096]{2,1,0:T(8,128)(2,1)}, u32[]{:S(2)}) copy-start(bf16[2,128,4096]{2,1,0:T(8,128)(2,1)} %param.11) | copy-start | bytes 6291460
  3.6 4.5 %copy-start.2 = (bf16[1,512,4,512]{3,2,1,0:T(4,128)(2,1)S(1)}, bf16[1,512,4,512]{3,2,1,0:T(4,128)(2,1)}, u32[]{:S(2)}) copy-start(bf16[1,512,4,512]{3,2,1,0:T(4,128)(2,1)} %param.10) | copy-start | bytes 6291460

commit v4 on v3

--- a/solution.py
+++ b/solution.py
@@ -139,14 +139,18 @@
         if j > 0:
             self.far_on(j - 1)
 
-    def close(self):
+    def finish(self, j):
+        for kind in range(4, 8):
+            self.into(j, kind).wait_recv()
+        self.keep(j).wait()
+
+    def close(self, finished=0):
         self.far_on(self.n - 1)
+        for j in range(finished, self.n):
+            self.finish(j)
         for j in range(self.n):
-            for kind in range(4, 8):
-                self.into(j, kind).wait_recv()
             for kind in range(8):
                 self.out(j, kind).wait_send()
-            self.keep(j).wait()
 
 
 class MpGather:
@@ -257,9 +261,9 @@
     return ref.at[pl.ds(rows, CH), cols]
 
 
-def gather_kernel(wt, xa, xb, full, slices, turn, w_send, w_recv, w_loc, t_send, t_recv, t_loc, b_send, b_recv, b_loc):
+def gather_kernel(wt, rows_in, gain, full, normed, q_ref, k_ref, v_ref, wbuf, w_sem, w_send, w_recv, w_loc):
     s, d, m = coords()
-    greet(mp_near(s, d, m) + dp_near(s, d, m), (d != m, (s, m, d)))
+    greet(dp_near(s, d, m))
     gather = DpGather(
         4,
         lambda j: wt.at[j],
@@ -269,62 +273,67 @@
         w_recv,
         w_loc,
     )
-    slots = [
-        SliceGather(
-            piece(ref, m),
-            turn.at[i],
-            slices.at[i],
-            t_send.at[i],
-            t_recv.at[i],
-            t_loc.at[i],
-            b_send.at[i],
-            b_recv.at[i],
-            b_loc.at[i],
-        )
-        for i, ref in enumerate((xa, xb))
-    ]
     gather.open()
-    slots[0].open()
-    pl.when(s == 1)(slots[1].open)
-    slots[0].middle()
-    pl.when(s == 1)(slots[1].middle)
+
+    @pl.loop(0, ROWS // 32)
+    def _(i):
+        rows = pl.ds(pl.multiple_of(i * 32, 32), 32)
+        value = rows_in[rows].astype(F32)
+        inverse = lax.rsqrt(jnp.mean(value * value, axis=-1, keepdims=True) + 1e-06)
+        normed[rows] = (value * inverse * gain[...].astype(F32)).astype(BF16)
+
+    outs = (q_ref, k_ref, v_ref)
+
+    def load(j):
+        return pltpu.make_async_copy(full.at[j], wbuf.at[j % 2], w_sem.at[j % 2])
+
+    def compute(j):
+        load(j).wait()
+
+        @pl.loop(0, 2)
+        def _(half):
+            cols = pl.ds(pl.multiple_of(half * 256, 256), 256)
+            acc = jnp.zeros((ROWS, 256), F32)
+            for b in range(N):
+                acc = acc + dot_nn(normed[:, b * PIECE : b * PIECE + PIECE], wbuf[j % 2, b, :, cols])
+            outs[j][:, cols] = acc.astype(BF16)
+
     gather.middle(0)
-    slots[0].second()
-    pl.when(s == 1)(slots[1].second)
-    gather.middle(1)
-    slots[0].third()
-    pl.when(s == 1)(slots[1].third)
-    for j in range(2, 4):
-        gather.middle(j)
-    gather.close()
-    slots[0].close()
-    pl.when(s == 1)(slots[1].close)
-
-
-def gather_weights(wt, xa, xb):
+    for j in range(3):
+        gather.middle(j + 1)
+        gather.finish(j)
+
+        @pl.when(s == 0)
+        def _():
+            load(j).start()
+            compute(j)
+
+    gather.close(3)
+
+
+def gather_weights(wt, rows_in, gain):
+    thin = jax.ShapeDtypeStruct((ROWS, PIECE), BF16)
     return pl.pallas_call(
         gather_kernel,
         name="gather_weights",
         out_shape=(
             jax.ShapeDtypeStruct((4, N, PIECE, PIECE), BF16),
-            jax.ShapeDtypeStruct((3, N * ROWS, PIECE), BF16),
+            jax.ShapeDtypeStruct((ROWS, D), BF16),
+            thin,
+            thin,
+            thin,
         ),
-        in_specs=[VM, ANY, ANY],
-        out_specs=(HBM, HBM),
+        in_specs=[VM, VM, VM],
+        out_specs=(HBM, VM, VM, VM, VM),
         scratch_shapes=[
-            pltpu.VMEM((2, ROWS, PIECE), BF16),
+            pltpu.VMEM((2, N, PIECE, PIECE), BF16),
+            DMA((2,)),
             DMA((4, 8)),
             DMA((4, 8)),
             DMA((4,)),
-            DMA((2,)),
-            DMA((2,)),
-            DMA((2,)),
-            DMA((2, SLICE_CHUNKS, 7)),
-            DMA((2, SLICE_CHUNKS, 7)),
-            DMA((2, SLICE_CHUNKS)),
         ],
         compiler_params=pltpu.CompilerParams(collective_id=0, has_side_effects=True),
-    )(wt, xa, xb)
+    )(wt, rows_in, gain)
 
 
 class Relay:
@@ -437,12 +446,28 @@
 
 
 def bridge_kernel(
-    lens, q_ref, k_in, v_in, g_in, resid, xa, xb, mats, ctx_ref, gq_ref, gk_ref, gv_ref, total, norm, rights, *rest
+    lens, q_in, k_in, v_in, rows_in, xa, cot, mats, ctx_ref, gq_ref, gk_ref, gv_ref, total, norm, rights, slices, *rest
 ):
     s, d, m = coords()
-    greet(mp_near(s, d, m) + dp_near(s, d, m) + [(1 - s, d, (m + 4) % N)])
+    greet(mp_near(s, d, m) + dp_near(s, d, m) + [(1 - s, d, (m + 4) % N)], (d != m, (s, m, d)))
     bufs, sems = rest[:9], rest[9:14]
-    y_send, y_recv, y_loc, w_sem, wbuf, terms, k_mid, v_mid, g_mid, gram_a, gram_b = rest[14:]
+    (y_send, y_recv, y_loc, w_sem, wbuf, terms, q_mid, k_mid, v_mid, g_mid, gram_a, gram_b) = rest[14:26]
+    xb, resid, r_sem, turn, t_send, t_recv, t_loc, b_send, b_recv, b_loc = rest[26:]
+
+    def slot(i, ref):
+        return SliceGather(
+            piece(ref, m),
+            turn.at[i],
+            slices.at[i],
+            t_send.at[i],
+            t_recv.at[i],
+            t_loc.at[i],
+            b_send.at[i],
+            b_recv.at[i],
+            b_loc.at[i],
+        )
+
+    slot_a, slot_b = slot(0, xa), slot(1, xb)
     relay = Relay(terms, resid, total, bufs, sems)
     gather = DpGather(
         1,
@@ -494,31 +519,39 @@
         @pl.loop(0, 2)
         def _(e):
             rows = pl.ds(pl.multiple_of(e * 128, 128), 128)
-            key_ok = lax.broadcasted_iota(jnp.int32, (128, 128), 1) < lens[e]
+            key_ok = lax.broadcasted_iota(jnp.int32, (128, 128), 1) < lens[0, e]
             for pair in range(4):
                 body(rows, slice(pair * 128, pair * 128 + 128), key_ok)
 
     @pl.when(s == 0)
     def _():
         load(3, 0).start()
+        bring = pltpu.make_async_copy(piece(rows_in, m), resid, r_sem)
+        bring.start()
 
         def ahead(rows, cols, key_ok):
-            ctx_ref[rows, cols] = context(q_ref[rows, cols], k_in[rows, cols], v_in[rows, cols], key_ok)
+            ctx_ref[rows, cols] = context(q_in[rows, cols], k_in[rows, cols], v_in[rows, cols], key_ok)
 
         each_head(ahead)
         gather.open()
         load(3, 0).wait()
+        bring.wait()
         send_terms(lambda index: dot_nt(ctx_ref[...], block(0, index)))
         relay.sender(True)
+        slot_a.open()
         gather.middle(0)
+        slot_a.middle()
         grams(xa, gram_a)
+        slot_a.second()
         gather.close()
+        slot_a.third()
+        slot_a.close()
         relay.taker()
         wide_dot(total, 0, g_mid)
 
         def back(rows, cols, key_ok):
             _, gq, gk, gv = gradients(
-                q_ref[rows, cols], k_in[rows, cols], v_in[rows, cols], g_mid[rows, cols], key_ok, False
+                q_in[rows, cols], k_in[rows, cols], v_in[rows, cols], g_mid[rows, cols], key_ok, False
             )
             gq_ref[rows, cols], gk_ref[rows, cols], gv_ref[rows, cols] = gq, gk, gv
 
@@ -533,10 +566,29 @@
 
     @pl.when(s == 1)
     def _():
+        load(0, 0).start()
+        load(3, 1).start()
+        slot_a.open()
+
+        @pl.loop(0, ROWS // 32)
+        def _(i):
+            rows = pl.ds(pl.multiple_of(i * 32, 32), 32)
+            place = lax.rem(i, 4) * 32 + lax.broadcasted_iota(jnp.int32, (32, D), 0)
+            value = cot[rows]
+            xb[rows] = jnp.where(place < lens[1, i // 4], value, jnp.zeros_like(value))
+
+        slot_a.middle()
+        load(0, 0).wait()
+        load(3, 1).wait()
+        wide_dot(xa, 0, q_mid)
+        slot_a.second()
+        wide_dot(xb, 1, g_mid)
+        slot_a.third()
         load(1, 0).start()
         load(2, 1).start()
         grams(xa, gram_a)
         grams(xb, gram_b)
+        slot_a.close()
         load(1, 0).wait()
         load(2, 1).wait()
         relay.taker()
@@ -545,7 +597,7 @@
 
         def both(rows, cols, key_ok):
             ctx, gq, gk, gv = gradients(
-                q_ref[rows, cols], k_mid[rows, cols], v_mid[rows, cols], g_in[rows, cols], key_ok, True
+                q_mid[rows, cols], k_mid[rows, cols], v_mid[rows, cols], g_mid[rows, cols], key_ok, True
             )
             ctx_ref[rows, cols], gq_ref[rows, cols], gk_ref[rows, cols], gv_ref[rows, cols] = ctx, gq, gk, gv
 
@@ -553,7 +605,9 @@
         send_terms(lambda index: dot_nt(gk_ref[...], block(0, index)) + dot_nt(gv_ref[...], block(1, index)))
         gather.open()
         relay.sender(False)
+        slot_b.open()
         gather.middle(0)
+        slot_b.middle()
 
         def value_of(e):
             rows = total[pl.ds(e * 128, 128)]
@@ -564,14 +618,18 @@
             )
 
         note(value_of)
+        slot_b.second()
         gather.close()
+        slot_b.third()
+        slot_b.close()
         relay.sender_close()
         relay.gather.close()
 
 
-def bridge(lens, q, k, v, g, resid, xa, xb, mats):
+def bridge(lens, q, k, v, rows_in, xa, cot, mats):
     thin = jax.ShapeDtypeStruct((ROWS, PIECE), BF16)
     small = pltpu.VMEM((ROWS, PIECE), BF16)
+    square = pltpu.VMEM((2, 128, 128), F32)
     return pl.pallas_call(
         bridge_kernel,
         name="bridge",
@@ -580,9 +638,10 @@
             jax.ShapeDtypeStruct((ROWS, D), BF16),
             jax.ShapeDtypeStruct((8, 128), F32),
             jax.ShapeDtypeStruct((4, N * ROWS, PIECE), BF16),
+            jax.ShapeDtypeStruct((3, N * ROWS, PIECE), BF16),
         ),
-        in_specs=[SM] + [VM] * 7 + [HBM],
-        out_specs=(VM,) * 6 + (HBM,),
+        in_specs=[SM] + [VM] * 3 + [HBM, VM, VM, HBM],
+        out_specs=(VM,) * 6 + (HBM, HBM),
         scratch_shapes=RELAY_BUFS
         + RELAY_SEMS
         + [
@@ -595,11 +654,22 @@
             small,
             small,
             small,
-            pltpu.VMEM((2, 128, 128), F32),
-            pltpu.VMEM((2, 128, 128), F32),
+            small,
+            square,
+            square,
+            pltpu.VMEM((ROWS, D), BF16),
+            small,
+            DMA,
+            pltpu.VMEM((2, ROWS, PIECE), BF16),
+            DMA((2,)),
+            DMA((2,)),
+            DMA((2,)),
+            DMA((2, SLICE_CHUNKS, 7)),
+            DMA((2, SLICE_CHUNKS, 7)),
+            DMA((2, SLICE_CHUNKS)),
         ],
         compiler_params=pltpu.CompilerParams(collective_id=1, has_side_effects=True),
-    )(lens, q, k, v, g, resid, xa, xb, mats)
+    )(lens, q, k, v, rows_in, xa, cot, mats)
 
 
 def final_kernel(
@@ -803,41 +873,15 @@
     )(sec, clip, slices, rights, dp_noise)
 
 
-def rms_norm(values_in, gain_row):
-    value32 = values_in.astype(F32)
-    inverse = lax.rsqrt(jnp.mean(value32 * value32, axis=-1, keepdims=True) + 1e-06)
-    return (value32 * inverse * gain_row.astype(F32)).astype(BF16)
-
-
-def project(left, right):
-    return jnp.dot(left, right, preferred_element_type=F32).astype(BF16)
-
-
 def per_device(inputs, norm_gains, weights, cotangent, lengths, dp_noise):
-    section = lax.axis_index("section")
-    is_dec = section == 1
-    sec = jnp.reshape(section, (1,)).astype(jnp.int32)
-    own_inputs = inputs[0].reshape(ROWS, D)
-    normed = rms_norm(own_inputs, norm_gains[0])
-    positions = jnp.arange(128)
-    keep = (positions[None, :] < lengths[1][:, None]).astype(BF16)
-    gout = (cotangent * keep[:, :, None]).reshape(ROWS, D)
+    sec = jnp.reshape(lax.axis_index("section"), (1,)).astype(jnp.int32)
+    rows_in = inputs[0].reshape(ROWS, D)
     wt = jnp.swapaxes(weights[0], 0, 1)
-    full, slices = gather_weights(wt, normed, gout)
+    full, normed, q, k, v = gather_weights(wt, rows_in, norm_gains)
     mats = full.reshape(4, D, PIECE)
-    lens = lengths[0]
-    thin = jnp.zeros((ROWS, PIECE), BF16)
-
-    def first_dec():
-        return project(normed, mats[0]), thin, thin, project(gout, mats[3])
-
-    def first_enc():
-        q, k, v = (project(normed, mats[i]) for i in range(3))
-        return q, k, v, thin
-
-    q, k, v, gctx = lax.cond(is_dec, first_dec, first_enc)
-    own_piece = lax.dynamic_slice_in_dim(own_inputs, lax.axis_index("mp") * PIECE, PIECE, 1)
-    ctx, gq, gk, gv, relayed, norm, rights = bridge(lens, q, k, v, gctx, own_piece, normed, gout, mats)
+    ctx, gq, gk, gv, relayed, norm, rights, slices = bridge(
+        lengths, q, k, v, rows_in, normed, cotangent.reshape(ROWS, D), mats
+    )
     slices, rights, norms = gather_grads(gq, gk, gv, relayed, norm, slices, rights)
     sq_norm = norms[:, 0, :2]
     bound = jnp.sqrt(jnp.float32(8.0 * D * HEADS * HEAD))

time: 296 us -> 288 us (0.973)
  the two profiles are of different devices: /device:TPU:1 before, /device:TPU:17 now
where the time goes in v4:
time: 288 us
  Pallas kernels  281 us (98%)
  local copies, waits for them, and re-layouts  4.96 us (2%)
    pallas_call x1, Pallas kernels, bridge(): pl.pallas_call(bridge_kernel, name='bridge', out_shape=(thin,) * 4 + (jax...  112 us
    pallas_call x1, Pallas kernels, gather_weights(): pl.pallas_call(gather_kernel, name='gather_weights', out_shape=(jax.Shape...  80.2 us
    pallas_call x1, Pallas kernels, gather_grads(): pl.pallas_call(final_kernel, name='gather_grads', out_shape=(jax.ShapeDty...  75.1 us
    pallas_call x1, Pallas kernels, weight_grads(): pl.pallas_call(weight_kernel, name='weight_grads', grid=(PIECE // BLOCK,)...  13.6 us

profile of v4, /device:TPU:17, one launch (start us, length us, event | category | flops | bytes accessed | tf_op | source)
XLA Modules:
  0.0 287.9 jit_solution(13268148094274147087)
XLA Ops:
  0.6 3.3 %copy.13 = bf16[1,512,4,512]{3,1,2,0:T(8,128)(2,1)} copy(bf16[1,512,4,512]{3,2,1,0:T(4,128)(2,1)} %param.8) | data formatting | bytes 4194304 | tf_op args[2]
  3.9 80.2 %gather_weights.1 = (bf16[4,8,512,512]{3,2,1,0:T(8,128)(2,1)}, bf16[256,4096]{1,0:T(8,128)(2,1)}, bf16[256,512]{1,0:T(8,128)(2,1)}, bf16[256,512]{1,0:T(8,128)(2,1)}, bf16[256,512]{1,0:T(8,128)(2,1)}) custom-call(bf16[4,512,512]{2,1,0:T(8,128)(2,1)} %bitcast.16, bf16[256,4096]{1,0:T(8,128)(2,1)} %bitcast.14, bf16[1,4096]{1,0:T(2,128)(2,1)} %gain.1), custom_call_target="tpu_custom_call" | custom-call | tf_op jit(solution)/shard_map/gather_weights/pallas_call | solution.py:316
  84.2 111.9 %bridge.1 = (bf16[256,512]{1,0:T(8,128)(2,1)}, bf16[256,512]{1,0:T(8,128)(2,1)}, bf16[256,512]{1,0:T(8,128)(2,1)}, bf16[256,512]{1,0:T(8,128)(2,1)}, bf16[256,40...) custom-call(s32[2,2]{1,0:T(2,128)} %lens.1, ...), custom_call_target="tpu_custom_call" | custom-call | tf_op jit(solution)/shard_map/bridge/pallas_call | solution.py:633
  196.1 75.1 %gather_grads.1 = (bf16[3,2048,512]{2,1,0:T(8,128)(2,1)}, bf16[4,2048,512]{2,1,0:T(8,128)(2,1)}, f32[8,8,128]{2,1,0:T(8,128)}) custom-call(bf16[256,512]{1,0:T(8,128)(2,1)} %get-tuple-element.22.gq, bf16[256,512]{1,0:T(8,128)(2,1)} %get-tuple-element.23.gk, bf16[256,512]{1,0:T(8,128)(2,1)} %get-tuple-element.24.gv, ...), custom_call_target="tpu_custom_call", output_to_operand_aliasing={{0}: (5, {}), {1}: (6, {})} | custom-call | tf_op jit(solution)/shard_map/gather_grads/pallas_call | solution.py:748
  271.2 0.5 broadcast.23
  271.7 1.4 fusion
  273.2 0.6 div.9.clip
  273.8 13.6 %weight_grads.1 = f32[512,4,512]{2,1,0:T(4,128)} custom-call(s32[1]{0:T(128)} %bitcast.sec, f32[16]{0:T(128)} %div.9.clip, bf16[3,2048,512]{2,1,0:T(8,128)(2,1)} %get-tuple-element.30.x_ref, bf16[4,2048,512]{2,1,0:T(8,128)(2,1)} %get-tuple-element.31.y_ref, f32[512,4,512]{2,1,0:T(4,128)} %bitcast.17), custom_call_target="tpu_custom_call" | custom-call | tf_op jit(solution)/shard_map/weight_grads/pallas_call | solution.py:859
  287.4 0.5 dynamic-slice_bitcast_fusion

commit v5 on v4

--- a/solution.py
+++ b/solution.py
@@ -16,7 +16,7 @@
 N = 8
 ROWS = 256
 PIECE = 512
-CHUNKS = 8
+CHUNKS = 4
 CH = ROWS // CHUNKS
 ANY = pl.BlockSpec(memory_space=pl.ANY)
 HBM = pl.BlockSpec(memory_space=pltpu.HBM)
@@ -577,18 +577,15 @@
             value = cot[rows]
             xb[rows] = jnp.where(place < lens[1, i // 4], value, jnp.zeros_like(value))
 
+        slot_b.open()
         slot_a.middle()
         load(0, 0).wait()
         load(3, 1).wait()
         wide_dot(xa, 0, q_mid)
         slot_a.second()
         wide_dot(xb, 1, g_mid)
-        slot_a.third()
         load(1, 0).start()
         load(2, 1).start()
-        grams(xa, gram_a)
-        grams(xb, gram_b)
-        slot_a.close()
         load(1, 0).wait()
         load(2, 1).wait()
         relay.taker()
@@ -605,9 +602,12 @@
         send_terms(lambda index: dot_nt(gk_ref[...], block(0, index)) + dot_nt(gv_ref[...], block(1, index)))
         gather.open()
         relay.sender(False)
-        slot_b.open()
+        slot_b.middle()
+        slot_a.third()
         gather.middle(0)
-        slot_b.middle()
+        slot_a.close()
+        grams(xa, gram_a)
+        grams(xb, gram_b)
 
         def value_of(e):
             rows = total[pl.ds(e * 128, 128)]

time: 288 us -> 269 us (0.934)
  the two profiles are of different devices: /device:TPU:17 before, /device:TPU:1 now
where the time goes in v5:
time: 269 us; the launch traced here: 267 us
  Pallas kernels  260 us (97%)
  local copies, waits for them, and re-layouts  4.96 us (2%)
    pallas_call x1, Pallas kernels, bridge(): pl.pallas_call(bridge_kernel, name='bridge', out_shape=(thin,) * 4 + (jax...  107 us
    pallas_call x1, Pallas kernels, gather_weights(): pl.pallas_call(gather_kernel, name='gather_weights', out_shape=(jax.Shape...  81.1 us
    pallas_call x1, Pallas kernels, gather_grads(): pl.pallas_call(final_kernel, name='gather_grads', out_shape=(jax.ShapeDty...  58.4 us
    pallas_call x1, Pallas kernels, weight_grads(): pl.pallas_call(weight_kernel, name='weight_grads', grid=(PIECE // BLOCK,)...  13.6 us

profile of v5, /device:TPU:1, one launch (start us, length us, event | category | flops | bytes accessed | tf_op | source)
XLA Modules:
  0.0 267.3 jit_solution(12887121709022118251)
XLA Ops:
  0.6 3.3 %copy.13 = bf16[1,512,4,512]{3,1,2,0:T(8,128)(2,1)} copy(bf16[1,512,4,512]{3,2,1,0:T(4,128)(2,1)} %param.8) | data formatting | bytes 4194304 | tf_op args[2]
  3.9 81.1 %gather_weights.1 = (bf16[4,8,512,512]{3,2,1,0:T(8,128)(2,1)}, bf16[256,4096]{1,0:T(8,128)(2,1)}, bf16[256,512]{1,0:T(8,128)(2,1)}, bf16[256,512]{1,0:T(8,128)(2,1)}, bf16[256,512]{1,0:T(8,128)(2,1)}) custom-call(bf16[4,512,512]{2,1,0:T(8,128)(2,1)} %bitcast.16, bf16[256,4096]{1,0:T(8,128)(2,1)} %bitcast.14, bf16[1,4096]{1,0:T(2,128)(2,1)} %gain.1), custom_call_target="tpu_custom_call" | custom-call | tf_op jit(solution)/shard_map/gather_weights/pallas_call | solution.py:316
  85.0 107.2 %bridge.1 = (bf16[256,512]{1,0:T(8,128)(2,1)}, bf16[256,512]{1,0:T(8,128)(2,1)}, bf16[256,512]{1,0:T(8,128)(2,1)}, bf16[256,512]{1,0:T(8,128)(2,1)}, bf16[256,40...) custom-call(s32[2,2]{1,0:T(2,128)} %lens.1, ...), custom_call_target="tpu_custom_call" | custom-call | tf_op jit(solution)/shard_map/bridge/pallas_call | solution.py:633
  192.2 58.4 %gather_grads.1 = (bf16[3,2048,512]{2,1,0:T(8,128)(2,1)}, bf16[4,2048,512]{2,1,0:T(8,128)(2,1)}, f32[8,8,128]{2,1,0:T(8,128)}) custom-call(bf16[256,512]{1,0:T(8,128)(2,1)} %get-tuple-element.22.gq, bf16[256,512]{1,0:T(8,128)(2,1)} %get-tuple-element.23.gk, bf16[256,512]{1,0:T(8,128)(2,1)} %get-tuple-element.24.gv, ...), custom_call_target="tpu_custom_call", output_to_operand_aliasing={{0}: (5, {}), {1}: (6, {})} | custom-call | tf_op jit(solution)/shard_map/gather_grads/pallas_call | solution.py:748
  250.6 0.5 broadcast.23
  251.1 1.4 fusion
  252.6 0.6 div.9.clip
  253.2 13.6 %weight_grads.1 = f32[512,4,512]{2,1,0:T(4,128)} custom-call(s32[1]{0:T(128)} %bitcast.sec, f32[16]{0:T(128)} %div.9.clip, bf16[3,2048,512]{2,1,0:T(8,128)(2,1)} %get-tuple-element.30.x_ref, bf16[4,2048,512]{2,1,0:T(8,128)(2,1)} %get-tuple-element.31.y_ref, f32[512,4,512]{2,1,0:T(4,128)} %bitcast.17), custom_call_target="tpu_custom_call" | custom-call | tf_op jit(solution)/shard_map/weight_grads/pallas_call | solution.py:859
  266.7 0.5 dynamic-slice_bitcast_fusion
